TPU v7x, 32 devices: a whole 2x2x4 slice. The times are simulated.
32 devices in a mesh: tile: 8 (over z, x), group: 4 (over y, core).
Axes of the slice: x: 2, y: 2, z: 4, core: 2. Of those that a mesh axis runs over, the one named last changes fastest.
Arguments:
- features: bfloat16 [4, 512, 32, 256], P('group', 'tile'), may hold values from -6 to 6
- out_grad: bfloat16 [4, 96, 14, 14, 256], P('group', 'tile'), may hold values from -6 to 6
- pair_count: int32 [4, 8, 8], P('group'), may hold values from 0 to 2, as said below
- sample_grid: int32 [4, 8, 8, 2, 4, 14], P('group', 'tile'), may hold values from 0 to 62, as said below
- first_kernel: bfloat16 [3, 3, 256, 256], replicated, may hold values from -0.125 to 0.125
- second_kernel: bfloat16 [3, 3, 256, 256], replicated, may hold values from -0.125 to 0.125
Outputs:
- feature_grad: bfloat16 [4, 512, 32, 256], P('group', 'tile')
- first_grad: float32 [3, 3, 256, 256], replicated
- second_grad: float32 [3, 3, 256, 256], replicated
Inputs may be any that keep to these rules, and one draw needn't show every extreme that they name: Every entry is at most 2; in every scene each reader t has pair_count entries summing to exactly 12 over the owners, and every reader has some owner sending it exactly 2 regions. `sample_grid`: lower row indices are at most 62 and lower column indices at most 30; fractions lie in 0 to 15; along a slot's samples the positions (16 * lower index + fraction) ascend with a constant step of 8 to 64.
All inputs are finite; a program needn't handle non-finite values.
Results may differ from a plain program's by a relative error of at most 0.015.
Values may be sent and summed in bfloat16 or wider, within the bound.
No kernel may reach another device: no remote copies, remote signals or barrier semaphores. Data moves between devices by JAX's collectives and lax.ppermute only.
A program may use at most 256 MiB of HBM per device.

v0:
```python
import math

import jax
import jax.numpy as jnp
from jax import lax
from jax.sharding import PartitionSpec as P


def interp_weights(lower_index, fraction, extent):
    places = jnp.arange(extent, dtype=jnp.int32)
    upper_share = fraction.astype(jnp.float32) / 16.0
    lower_part = jnp.where(places == lower_index[..., None], 1.0 - upper_share[..., None], 0.0)
    upper_part = jnp.where(places == lower_index[..., None] + 1, upper_share[..., None], 0.0)
    return lower_part + upper_part


def column_weights(slot_grid, across):
    return interp_weights(slot_grid[..., 2, :], slot_grid[..., 3, :], across).astype(jnp.bfloat16)


def sample_blocks(tile_image, lower_rows, lower_weight, upper_weight, col_weights):
    leading = lower_rows.shape[:2]
    slot_total = leading[0] * leading[1]
    extent = lower_rows.shape[2]
    across = tile_image.shape[1]
    channels = tile_image.shape[2]
    low_blocks = lower_rows.reshape(slot_total // 8, 8, extent)
    lw_blocks = lower_weight.reshape(slot_total // 8, 8, extent)
    uw_blocks = upper_weight.reshape(slot_total // 8, 8, extent)
    col_blocks = col_weights.reshape(slot_total // 8, 8, extent, across)

    def sample_one_block(members):
        low_part, lw_part, uw_part, col_part = members
        lower_taken = jnp.take(tile_image, low_part, axis=0).astype(jnp.float32)
        upper_taken = jnp.take(tile_image, low_part + 1, axis=0).astype(jnp.float32)
        stripes = (
            lw_part.astype(jnp.float32)[..., None, None] * lower_taken
            + uw_part.astype(jnp.float32)[..., None, None] * upper_taken
        ).astype(jnp.bfloat16)
        return jnp.einsum(
            "sqx,spxc->spqc", col_part, stripes, preferred_element_type=jnp.float32
        ).astype(jnp.bfloat16)

    sampled = lax.map(sample_one_block, (low_blocks, lw_blocks, uw_blocks, col_blocks))
    return sampled.reshape(leading + (extent, extent, channels))


def spread_blocks(slot_grads, lower_rows, lower_weight, upper_weight, col_weights, height):
    leading = lower_rows.shape[:2]
    slot_total = leading[0] * leading[1]
    extent = lower_rows.shape[2]
    across = col_weights.shape[3]
    channels = slot_grads.shape[-1]
    low_blocks = lower_rows.reshape(slot_total // 8, 8, extent)
    lw_blocks = lower_weight.reshape(slot_total // 8, 8, extent)
    uw_blocks = upper_weight.reshape(slot_total // 8, 8, extent)
    col_blocks = col_weights.reshape(slot_total // 8, 8, extent, across)
    grad_blocks = slot_grads.reshape(slot_total // 8, 8, extent, extent, channels)

    def spread_one_block(running_sum, members):
        low_part, lw_part, uw_part, col_part, grad_part = members
        stripes = jnp.einsum(
            "sqx,spqc->spxc", col_part, grad_part, preferred_element_type=jnp.float32
        ).astype(jnp.bfloat16)
        stripes_wide = stripes.astype(jnp.float32)
        lower_terms = (lw_part.astype(jnp.float32)[..., None, None] * stripes_wide).reshape(
            -1, across, channels
        )
        upper_terms = (uw_part.astype(jnp.float32)[..., None, None] * stripes_wide).reshape(
            -1, across, channels
        )
        flat_rows = low_part.reshape(-1)
        running_sum = running_sum.at[flat_rows].add(lower_terms)
        running_sum = running_sum.at[flat_rows + 1].add(upper_terms)
        return (running_sum, None)

    initial = jnp.zeros((height, across, channels), jnp.float32)
    summed, unused = lax.scan(
        spread_one_block, initial, (low_blocks, lw_blocks, uw_blocks, col_blocks, grad_blocks)
    )
    return summed.astype(jnp.bfloat16)


def unfold(values):
    region_count = values.shape[0]
    extent = values.shape[1]
    channels = values.shape[3]
    padded = jnp.pad(values, ((0, 0), (1, 1), (1, 1), (0, 0)))
    pieces = [
        padded[:, row_off : row_off + extent, col_off : col_off + extent, :]
        for row_off in range(3)
        for col_off in range(3)
    ]
    return jnp.concatenate(pieces, axis=-1).reshape(region_count * extent * extent, 9 * channels)


def refold(columns, region_count, extent, channels):
    pieces = columns.reshape(region_count, extent, extent, 9, channels)
    padded = jnp.zeros((region_count, extent + 2, extent + 2, channels), jnp.float32)
    for row_off in range(3):
        for col_off in range(3):
            padded = padded.at[:, row_off : row_off + extent, col_off : col_off + extent, :].add(
                pieces[:, :, :, 3 * row_off + col_off, :]
            )
    return padded[:, 1:-1, 1:-1, :]


def silu_slope(values):
    sigma = jax.nn.sigmoid(values)
    return sigma * (1.0 + values * (1.0 - sigma))


def region_pass(inputs, upstream, first_kernel, second_kernel):
    region_count = inputs.shape[0]
    extent = inputs.shape[1]
    channels = inputs.shape[3]
    first_flat = first_kernel.reshape(9 * channels, channels)
    second_flat = second_kernel.reshape(9 * channels, channels)
    contract_rows = (((0,), (0,)), ((), ()))
    contract_last = (((1,), (1,)), ((), ()))
    input_cols = unfold(inputs)
    first_pre = jnp.dot(input_cols, first_flat, preferred_element_type=jnp.float32)
    hidden = jax.nn.silu(first_pre).astype(jnp.bfloat16)
    hidden_cols = unfold(hidden.reshape(region_count, extent, extent, channels))
    second_pre = jnp.dot(hidden_cols, second_flat, preferred_element_type=jnp.float32)
    second_delta = (
        upstream.reshape(-1, channels).astype(jnp.float32) * silu_slope(second_pre)
    ).astype(jnp.bfloat16)
    second_raw = lax.dot_general(
        hidden_cols, second_delta, contract_rows, preferred_element_type=jnp.float32
    )
    hidden_cols_back = lax.dot_general(
        second_delta, second_flat, contract_last, preferred_element_type=jnp.float32
    )
    hidden_back = refold(hidden_cols_back, region_count, extent, channels)
    first_delta = (hidden_back.reshape(-1, channels) * silu_slope(first_pre)).astype(jnp.bfloat16)
    first_raw = lax.dot_general(
        input_cols, first_delta, contract_rows, preferred_element_type=jnp.float32
    )
    input_cols_back = lax.dot_general(
        first_delta, first_flat, contract_last, preferred_element_type=jnp.float32
    )
    input_back = refold(input_cols_back, region_count, extent, channels).astype(jnp.bfloat16)
    return (input_back, first_raw, second_raw)


def compact_plan(active, region_total):
    live_flags = active.reshape(-1)
    running = jnp.cumsum(live_flags.astype(jnp.int32), dtype=jnp.int32)
    region_ids = jnp.arange(region_total, dtype=jnp.int32)
    chosen = jnp.sum(
        (running[None, :] <= region_ids[:, None]).astype(jnp.int32), axis=1, dtype=jnp.int32
    )
    placed = jnp.maximum(running - 1, 0)
    return (chosen, placed, live_flags)


def on_device(features, out_grad, pair_count, sample_grid, first_kernel, second_kernel):
    tile_count = lax.axis_size("tile")
    own_index = lax.axis_index("tile")
    tile_image = features[0]
    height = tile_image.shape[0]
    across = tile_image.shape[1]
    channels = tile_image.shape[2]
    counts = pair_count[0]
    slot_grid = sample_grid[0, 0]
    capacity = slot_grid.shape[1]
    extent = slot_grid.shape[3]
    upstream = out_grad[0]
    region_total = upstream.shape[0]
    slot_ids = jnp.arange(capacity, dtype=jnp.int32)
    send_counts = lax.dynamic_index_in_dim(counts, own_index, 0, keepdims=False)
    send_active = slot_ids[None, :] < send_counts[:, None]
    lower_rows = slot_grid[..., 0, :]
    upper_share = slot_grid[..., 1, :].astype(jnp.float32) / 16.0
    live_scale = send_active[..., None].astype(jnp.float32)
    lower_weight = ((1.0 - upper_share) * live_scale).astype(jnp.bfloat16)
    upper_weight = (upper_share * live_scale).astype(jnp.bfloat16)
    col_weights = column_weights(slot_grid, across)
    sent_blocks = sample_blocks(tile_image, lower_rows, lower_weight, upper_weight, col_weights)
    arrived = lax.all_to_all(sent_blocks, "tile", split_axis=0, concat_axis=0, tiled=True)
    recv_counts = lax.dynamic_index_in_dim(counts, own_index, 1, keepdims=False)
    recv_active = slot_ids[None, :] < recv_counts[:, None]
    chosen, placed, live_flags = compact_plan(recv_active, region_total)
    inputs = jnp.take(
        arrived.reshape(tile_count * capacity, extent, extent, channels), chosen, axis=0
    )
    input_back, first_raw, second_raw = region_pass(inputs, upstream, first_kernel, second_kernel)
    taken_back = jnp.take(input_back, placed, axis=0)
    slot_back = jnp.where(live_flags[:, None, None, None], taken_back, jnp.zeros_like(taken_back))
    slot_back = slot_back.reshape(tile_count, capacity, extent, extent, channels)
    returned = lax.all_to_all(slot_back, "tile", split_axis=0, concat_axis=0, tiled=True)
    image_grads = spread_blocks(
        returned, lower_rows, lower_weight, upper_weight, col_weights, height
    )
    shares = (
        lax.psum_scatter(
            first_raw.astype(jnp.bfloat16), "tile", scatter_dimension=0, tiled=True
        ).astype(jnp.float32),
        lax.psum_scatter(
            second_raw.astype(jnp.bfloat16), "tile", scatter_dimension=0, tiled=True
        ).astype(jnp.float32),
    )
    shares = (
        lax.psum(shares[0].astype(jnp.bfloat16), "group").astype(jnp.float32),
        lax.psum(shares[1].astype(jnp.bfloat16), "group").astype(jnp.float32),
    )
    first_total, second_total = (
        lax.all_gather(shares[0].astype(jnp.bfloat16), "tile", axis=0, tiled=True).astype(
            jnp.float32
        ),
        lax.all_gather(shares[1].astype(jnp.bfloat16), "tile", axis=0, tiled=True).astype(
            jnp.float32
        ),
    )
    grad_scale = 1.0 / math.sqrt(
        lax.axis_size("group") * tile_count * region_total * extent * extent
    )
    first_grad = (first_total * grad_scale).reshape(3, 3, channels, channels)
    second_grad = (second_total * grad_scale).reshape(3, 3, channels, channels)
    return (image_grads[None], first_grad, second_grad)


def solution(mesh):
    return jax.shard_map(
        on_device,
        mesh=mesh,
        in_specs=(
            P("group", "tile", None, None),
            P("group", "tile", None, None, None),
            P("group", None, None),
            P("group", "tile", None, None, None, None),
            P(),
            P(),
        ),
        out_specs=(P("group", "tile", None, None), P(), P()),
        check_vma=False,
    )
```

profile of v0, /device:TPU:0, one launch (start us, length us, event | category | flops | bytes accessed | tf_op | source)
XLA Modules:
  0.0 666.5 jit_solution(12716391202652129024)
XLA Ops:
  10.3 19.2 %while.40 = (s32[]{:T(128)}, bf16[2,8,14,14,256]{4,3,2,1,0:T(8,128)(2,1)}, bf16[2,8,14]{2,1,0:T(8,128)(2,1)S(1)}, s32[2,8,14]{2,1,0:T(8,128)S(1)}, bf16[64,32,25...) while((s32[]{:T(128)}, ...), condition=%wide.region_3.5_spmd, body=%wide.region_2.4_spmd.sunk | while | flops 33435280 | bytes 16180697 | solution.py:44
  50.0 29.8 %all-to-all-done = bf16[8,2,14,14,256]{4,1,3,2,0:T(2,128)(2,1)S(1)} async-done(((bf16[8,2,14,14,256]{4,1,3,2,0:T(2,128)(2,1)}), bf16[8,2,14,14,256]{4,1,3,2,0:T(2,128)(2,1)S(1)}, u32[]{:S(2)}, u32[]{:S(2)}) %all-to-all-start) | async-done | bytes 1605664 | tf_op jit(solution)/shard_map/all_to_all | solution.py:181
  98.2 16.7 %reshape.1063 = bf16[2352,2304]{1,0:T(8,128)(2,1)} reshape(bf16[12,14,14,2304]{3,2,1,0:T(8,128)(2,1)} %slice_dynamic-update-slice_fusion) | data formatting | bytes 21676032 | tf_op jit(solution)/shard_map/reshape | solution.py:94
  114.9 8.9 %multiply_convert_fusion.2 = (bf16[2352,256]{1,0:T(8,128)(2,1)S(1)}, f32[2352,256]{1,0:T(8,128)}) fusion(bf16[2352,2304]{1,0:T(8,128)(2,1)} %reshape.1063, bf16[2304,256]{1,0:T(8,128)(2,1)} %bitcast.225), kind=kOutput, calls=%fused_computation.87 | convolution fusion | flops 2777542656 | bytes 15630336 | tf_op jit(solution)/shard_map/dot_general | solution.py:122
  126.0 8.2 %pad_slice_fusion = (bf16[12,14,14,256]{3,2,1,0:T(8,128)(2,1)S(1)}, bf16[12,14,14,256]{3,2,1,0:T(8,128)(2,1)}, bf16[12,14,14,256]{3,2,1,0:T(8,128)(2,1)}, bf16[1...) fusion(bf16[12,14,14,256]{3,2,1,0:T(8,128)(2,1)} %reshape.1065), kind=kLoop, calls=%fused_computation.103 | loop fusion | bytes 10838016 | tf_op jit(solution)/shard_map/slice | solution.py:90
  172.1 9.4 %multiply_convert_fusion.1 = (bf16[2352,256]{1,0:T(8,128)(2,1)}, f32[2352,256]{1,0:T(8,128)}) fusion(f32[2352,256]{1,0:T(8,128)S(1)} %copy-done.13, bf16[2352,2304]{1,0:T(8,128)(2,1)} %constant_dynamic-update-slice_fusion.1, bf16[2304,256]{1,0:T(8,128)(2,1)S(1)} %bitcast.213), kind=kOutput, calls=%fused_computation.86 | convolution fusion | flops 2779951104 | bytes 18038784 | tf_op jit(solution)/shard_map/dot_general | solution.py:125
  199.8 11.7 %scatter-add.85 = f32[12,16,16,256]{3,2,1,0:T(8,128)} dynamic-update-slice(f32[12,16,16,256]{3,2,1,0:T(8,128)} %scatter-add.84, f32[12,14,14,256]{3,2,1,0:T(8,128)} %fusion.35, s32[]{:T(128)} %copy.209, s32[]{:T(128)} %bitcast.39, s32[]{:T(128)} %bitcast.40, s32[]{:T(128)} %copy.209) | dynamic-update-slice | bytes 4816900 | tf_op jit(solution)/shard_map/scatter-add | solution.py:102
  218.2 11.7 %scatter-add.86 = f32[12,16,16,256]{3,2,1,0:T(8,128)} dynamic-update-slice(f32[12,16,16,256]{3,2,1,0:T(8,128)} %scatter-add.85, f32[12,14,14,256]{3,2,1,0:T(8,128)} %add_select_fusion.1, s32[]{:T(128)} %copy.209, s32[]{:T(128)} %bitcast.42, s32[]{:T(128)} %bitcast.43, s32[]{:T(128)} %copy.209) | dynamic-update-slice | bytes 4816900 | tf_op jit(solution)/shard_map/scatter-add | solution.py:102
  234.7 10.4 %scatter-add.89 = f32[12,16,16,256]{3,2,1,0:T(8,128)} dynamic-update-slice(f32[12,16,16,256]{3,2,1,0:T(8,128)} %scatter-add.86, f32[12,14,14,256]{3,2,1,0:T(8,128)} %fusion.34, s32[]{:T(128)} %copy.209, s32[]{:T(128)} %constant.575.clone.1, s32[]{:T(128)} %copy.209, s32[]{:T(128)} %copy.209) | dynamic-update-slice | bytes 4816900 | tf_op jit(solution)/shard_map/scatter-add | solution.py:102
  249.8 10.6 %scatter-add.90 = f32[12,16,16,256]{3,2,1,0:T(8,128)} dynamic-update-slice(f32[12,16,16,256]{3,2,1,0:T(8,128)} %scatter-add.89, f32[12,14,14,256]{3,2,1,0:T(8,128)} %fusion.33, s32[]{:T(128)} %copy.209, s32[]{:T(128)} %constant.575.clone.1, s32[]{:T(128)} %constant.575.clone.1, s32[]{:T(128)} %copy.209) | dynamic-update-slice | bytes 4816900 | tf_op jit(solution)/shard_map/scatter-add | solution.py:102
  265.2 10.4 %scatter-add.91 = f32[12,16,16,256]{3,2,1,0:T(8,128)} dynamic-update-slice(f32[12,16,16,256]{3,2,1,0:T(8,128)} %scatter-add.90, f32[12,14,14,256]{3,2,1,0:T(8,128)} %fusion.32, s32[]{:T(128)} %copy.209, s32[]{:T(128)} %constant.575.clone.1, s32[]{:T(128)} %constant.583.clone.1, s32[]{:T(128)} %copy.209) | dynamic-update-slice | bytes 4816900 | tf_op jit(solution)/shard_map/scatter-add | solution.py:102
  280.4 10.4 %scatter-add.94 = f32[12,16,16,256]{3,2,1,0:T(8,128)} dynamic-update-slice(f32[12,16,16,256]{3,2,1,0:T(8,128)} %scatter-add.91, f32[12,14,14,256]{3,2,1,0:T(8,128)} %fusion.31, s32[]{:T(128)} %copy.209, s32[]{:T(128)} %constant.583.clone.1, s32[]{:T(128)} %copy.209, s32[]{:T(128)} %copy.209) | dynamic-update-slice | bytes 4816900 | tf_op jit(solution)/shard_map/scatter-add | solution.py:102
  295.5 10.4 %scatter-add.95 = f32[12,16,16,256]{3,2,1,0:T(8,128)} dynamic-update-slice(f32[12,16,16,256]{3,2,1,0:T(8,128)} %scatter-add.94, f32[12,14,14,256]{3,2,1,0:T(8,128)} %fusion.30, s32[]{:T(128)} %copy.209, s32[]{:T(128)} %constant.583.clone.1, s32[]{:T(128)} %constant.575.clone.1, s32[]{:T(128)} %copy.209) | dynamic-update-slice | bytes 4816900 | tf_op jit(solution)/shard_map/scatter-add | solution.py:102
  310.7 10.4 %scatter-add.96 = f32[12,16,16,256]{3,2,1,0:T(8,128)} dynamic-update-slice(f32[12,16,16,256]{3,2,1,0:T(8,128)} %scatter-add.95, f32[12,14,14,256]{3,2,1,0:T(8,128)} %fusion.29, s32[]{:T(128)} %copy.209, s32[]{:T(128)} %constant.583.clone.1, s32[]{:T(128)} %constant.583.clone.1, s32[]{:T(128)} %copy.209) | dynamic-update-slice | bytes 4816900 | tf_op jit(solution)/shard_map/scatter-add | solution.py:102
  350.0 8.6 %convolution_convert_fusion.1 = bf16[2304,256]{1,0:T(8,128)(2,1)} fusion(bf16[2352,2304]{1,0:T(8,128)(2,1)} %constant_dynamic-update-slice_fusion.1, f32[2352,256]{1,0:T(8,128)S(1)} %copy-done.14, f32[2352,256]{1,0:T(8,128)S(1)} %copy-done.28), kind=kOutput, calls=%fused_computation.48 | convolution fusion | flops 2780540928 | bytes 16834560 | tf_op jit(solution)/shard_map/dot_general | solution.py:129
  358.8 11.9 %scatter-add.120 = f32[12,16,16,256]{3,2,1,0:T(8,128)} dynamic-update-slice(f32[12,16,16,256]{3,2,1,0:T(8,128)} %scatter-add.99, f32[12,14,14,256]{3,2,1,0:T(8,128)} %fusion.28, s32[]{:T(128)} %copy.209, s32[]{:T(128)} %bitcast.39, s32[]{:T(128)} %bitcast.40, s32[]{:T(128)} %copy.209) | dynamic-update-slice | bytes 4816900 | tf_op jit(solution)/shard_map/scatter-add | solution.py:102
  377.5 11.7 %scatter-add.121 = f32[12,16,16,256]{3,2,1,0:T(8,128)} dynamic-update-slice(f32[12,16,16,256]{3,2,1,0:T(8,128)} %scatter-add.120, f32[12,14,14,256]{3,2,1,0:T(8,128)} %add_select_fusion, s32[]{:T(128)} %copy.209, s32[]{:T(128)} %bitcast.42, s32[]{:T(128)} %bitcast.43, s32[]{:T(128)} %copy.209) | dynamic-update-slice | bytes 4816900 | tf_op jit(solution)/shard_map/scatter-add | solution.py:102
  394.1 10.5 %scatter-add.122 = f32[12,16,16,256]{3,2,1,0:T(8,128)} dynamic-update-slice(f32[12,16,16,256]{3,2,1,0:T(8,128)} %scatter-add.121, f32[12,14,14,256]{3,2,1,0:T(8,128)} %fusion.27, s32[]{:T(128)} %copy.209, s32[]{:T(128)} %constant.575.clone.1, s32[]{:T(128)} %copy.209, s32[]{:T(128)} %copy.209) | dynamic-update-slice | bytes 4816900 | tf_op jit(solution)/shard_map/scatter-add | solution.py:102
  409.3 10.4 %scatter-add.123 = f32[12,16,16,256]{3,2,1,0:T(8,128)} dynamic-update-slice(f32[12,16,16,256]{3,2,1,0:T(8,128)} %scatter-add.122, f32[12,14,14,256]{3,2,1,0:T(8,128)} %fusion.26, s32[]{:T(128)} %copy.209, s32[]{:T(128)} %constant.575.clone.1, s32[]{:T(128)} %constant.575.clone.1, s32[]{:T(128)} %copy.209) | dynamic-update-slice | bytes 4816900 | tf_op jit(solution)/shard_map/scatter-add | solution.py:102
  424.6 10.4 %scatter-add.124 = f32[12,16,16,256]{3,2,1,0:T(8,128)} dynamic-update-slice(f32[12,16,16,256]{3,2,1,0:T(8,128)} %scatter-add.123, f32[12,14,14,256]{3,2,1,0:T(8,128)} %fusion.25, s32[]{:T(128)} %copy.209, s32[]{:T(128)} %constant.575.clone.1, s32[]{:T(128)} %constant.583.clone.1, s32[]{:T(128)} %copy.209) | dynamic-update-slice | bytes 4816900 | tf_op jit(solution)/shard_map/scatter-add | solution.py:102
  439.9 10.5 %scatter-add.125 = f32[12,16,16,256]{3,2,1,0:T(8,128)} dynamic-update-slice(f32[12,16,16,256]{3,2,1,0:T(8,128)} %scatter-add.124, f32[12,14,14,256]{3,2,1,0:T(8,128)} %fusion.24, s32[]{:T(128)} %copy.209, s32[]{:T(128)} %constant.583.clone.1, s32[]{:T(128)} %copy.209, s32[]{:T(128)} %copy.209) | dynamic-update-slice | bytes 4816900 | tf_op jit(solution)/shard_map/scatter-add | solution.py:102
  450.4 8.4 %convolution_convert_fusion.2 = bf16[2304,256]{1,0:T(8,128)(2,1)} fusion(bf16[2352,2304]{1,0:T(8,128)(2,1)} %reshape.1063, bf16[2352,256]{1,0:T(8,128)(2,1)S(1)} %copy-done.12), kind=kOutput, calls=%fused_computation.49 | convolution fusion | flops 2775121920 | bytes 13221888 | tf_op jit(solution)/shard_map/dot_general | solution.py:137
  463.7 10.4 %scatter-add.126 = f32[12,16,16,256]{3,2,1,0:T(8,128)} dynamic-update-slice(f32[12,16,16,256]{3,2,1,0:T(8,128)} %scatter-add.125, f32[12,14,14,256]{3,2,1,0:T(8,128)} %fusion.23, s32[]{:T(128)} %copy.209, s32[]{:T(128)} %constant.583.clone.1, s32[]{:T(128)} %constant.575.clone.1, s32[]{:T(128)} %copy.209) | dynamic-update-slice | bytes 4816900 | tf_op jit(solution)/shard_map/scatter-add | solution.py:102
  479.1 10.7 %scatter-add.127 = f32[12,16,16,256]{3,2,1,0:T(8,128)} dynamic-update-slice(f32[12,16,16,256]{3,2,1,0:T(8,128)} %scatter-add.126, f32[12,14,14,256]{3,2,1,0:T(8,128)} %fusion.22, s32[]{:T(128)} %copy.209, s32[]{:T(128)} %constant.583.clone.1, s32[]{:T(128)} %constant.583.clone.1, s32[]{:T(128)} %copy.209) | dynamic-update-slice | bytes 4816900 | tf_op jit(solution)/shard_map/scatter-add | solution.py:102
  502.5 24.4 %reduce-scatter.3.cloned.1.call-done = bf16[288,256]{1,0:T(8,128)(2,1)} async-done(((bf16[2304,256]{1,0:T(8,128)(2,1)}), bf16[288,256]{1,0:T(8,128)(2,1)}) %reduce-scatter.3.cloned.1.call-update) | async-done | bytes 147472 | tf_op jit(solution)/shard_map/reduce_scatter | solution.py:197
  527.0 44.5 %all-reduce.7.cloned.1.call-done = (bf16[288,256]{1,0:T(8,128)(2,1)}, bf16[288,256]{1,0:T(8,128)(2,1)}) async-done(((bf16[288,256]{1,0:T(8,128)(2,1)}, bf16[288,256]{1,0:T(8,128)(2,1)}), (bf16[288,256]{1,0:T(8,128)(2,1)}, bf16[288,256]{1,0:T(8,128)(2,1)})) %all-reduce.7.cloned.1.call-update) | async-done | bytes 294928 | tf_op jit(solution)/shard_map/psum | solution.py:205
  574.0 57.8 %while.41 = (s32[]{:T(128)}, f32[64,32,256]{2,1,0:T(8,128)S(1)}, s32[2,8,14]{2,1,0:T(8,128)S(1)}, bf16[2,8,14]{2,1,0:T(8,128)(2,1)S(1)}, bf16[2,8,14,14,256]{4,3...) while((s32[]{:T(128)}, f32[64,32,256]{2,1,0:T(8,128)S(1)}, ...), condition=%wide.region_8.10_spmd, body=%wide.region_5.9_spmd.sunk | while | flops 31196144 | bytes 30325084 | solution.py:78
  579.1 11.9 %scatter_fusion = f32[64,32,256]{2,1,0:T(8,128)S(1)} fusion(f32[64,32,256]{2,1,0:T(8,128)S(1)} %get-tuple-element.581, s32[112]{0:T(128)S(1)} %get-tuple-element.542, f32[112,32,256]{2,1,0:T(8,128)} %bitcast.215), kind=kCustom, calls=%fused_computation.4.clone.1 | custom fusion | flops 917504 | bytes 11010496 | tf_op jit(solution)/shard_map/while/body/eval_jaxpr/scatter-add | solution.py:73
  591.0 12.0 %scatter_fusion.1 = f32[64,32,256]{2,1,0:T(8,128)S(1)} fusion(f32[64,32,256]{2,1,0:T(8,128)S(1)} %scatter_fusion, s32[112]{0:T(128)S(1)} %get-tuple-element.546, f32[112,32,256]{2,1,0:T(8,128)} %bitcast.214), kind=kCustom, calls=%fused_computation.5.clone.1 | custom fusion | flops 917504 | bytes 11010496 | tf_op jit(solution)/shard_map/while/body/eval_jaxpr/scatter-add | solution.py:74
  608.1 11.8 %scatter_fusion = f32[64,32,256]{2,1,0:T(8,128)S(1)} fusion(f32[64,32,256]{2,1,0:T(8,128)S(1)} %get-tuple-element.581, s32[112]{0:T(128)S(1)} %get-tuple-element.542, f32[112,32,256]{2,1,0:T(8,128)} %bitcast.215), kind=kCustom, calls=%fused_computation.4.clone.1 | custom fusion | flops 917504 | bytes 11010496 | tf_op jit(solution)/shard_map/while/body/eval_jaxpr/scatter-add | solution.py:73
  619.9 11.9 %scatter_fusion.1 = f32[64,32,256]{2,1,0:T(8,128)S(1)} fusion(f32[64,32,256]{2,1,0:T(8,128)S(1)} %scatter_fusion, s32[112]{0:T(128)S(1)} %get-tuple-element.546, f32[112,32,256]{2,1,0:T(8,128)} %bitcast.214), kind=kCustom, calls=%fused_computation.5.clone.1 | custom fusion | flops 917504 | bytes 11010496 | tf_op jit(solution)/shard_map/while/body/eval_jaxpr/scatter-add | solution.py:74
  635.9 20.7 %all-gather.5.cloned.1.call-done = bf16[2304,256]{1,0:T(8,128)(2,1)} async-done(((bf16[288,256]{1,0:T(8,128)(2,1)}), bf16[2304,256]{1,0:T(8,128)(2,1)}) %all-gather.5.cloned.1.call-update) | async-done | bytes 1179664 | tf_op jit(solution)/shard_map/all_gather | solution.py:212
  (204 shorter events, 251.9 us)
Async XLA Ops:
  7.2 165.0 %copy-start = (bf16[3,3,256,256]{3,2,1,0:T(8,128)(2,1)S(1)}, bf16[3,3,256,256]{3,2,1,0:T(8,128)(2,1)}, u32[]{:S(2)}) copy-start(bf16[3,3,256,256]{3,2,1,0:T(8,128)(2,1)} %param.53) | copy-start | bytes 3538948
  10.3 3.5 copy-start.2
  19.9 3.5 copy-start.2
  29.6 5.2 copy-start.16
  29.6 5.2 copy-start.18
  29.6 5.2 copy-start.20
  29.6 5.2 copy-start.22
  34.7 7.6 %copy-start.25 = (s32[1,8,8]{2,1,0:T(8,128)S(1)}, s32[1,8,8]{2,1,0:T(8,128)}, u32[]{:S(2)}) copy-start(s32[1,8,8]{2,1,0:T(8,128)} %param.50) | copy-start | bytes 772
  34.8 45.0 %all-to-all-start = ((bf16[8,2,14,14,256]{4,1,3,2,0:T(2,128)(2,1)}), bf16[8,2,14,14,256]{4,1,3,2,0:T(2,128)(2,1)S(1)}, u32[]{:S(2)}, u32[]{:S(2)}) async-start(bf16[8,2,14,14,256]{4,1,3,2,0:T(2,128)(2,1)} %copy.115), calls=%async_computation | async-start | bytes 3211264 | tf_op jit(solution)/shard_map/all_to_all | solution.py:181
  42.0 7.2 %copy-start.27 = (s32[4]{0:T(128)S(1)}, s32[4]{0:T(128)}, u32[]{:S(2)}) copy-start(s32[4]{0:T(128)} %constant.584.clone.1) | copy-start | bytes 52
  42.1 460.5 %reduce-scatter.5.cloned.1.call-start = ((), (), s32[]{:S(2)}) async-start(), calls=%async_computation.6 | async-start | bytes 1327104 | tf_op jit(solution)/shard_map/reduce_scatter | solution.py:200
  148.9 2.6 copy-start.11
  148.9 3.9 copy-start.10
  151.5 2.4 copy-start.6
  165.9 2.6 copy-start.9
  165.9 3.8 copy-start.7
  168.6 2.3 copy-start.8
  169.7 2.4 copy-start.13
  187.1 9.1 %copy-start.4 = (f32[12,14,14,9,256]{4,2,3,1,0:T(8,128)}, f32[12,14,14,9,256]{4,2,3,1,0:T(8,128)S(1)}, u32[]{:S(2)}) copy-start(f32[12,14,14,9,256]{4,2,3,1,0:T(8,128)S(1)} %fusion.36) | copy-start | bytes 65028100
  332.6 2.3 copy-start.15
  338.3 11.7 %copy-start.3 = (f32[12,14,14,9,256]{4,2,1,0,3:T(8,128)}, f32[12,14,14,9,256]{4,2,1,0,3:T(8,128)S(1)}, u32[]{:S(2)}) copy-start(f32[12,14,14,9,256]{4,2,1,0,3:T(8,128)S(1)} %fusion.47) | copy-start | bytes 65028100
  342.9 7.2 %copy-start.14 = (f32[2352,256]{1,0:T(8,128)S(1)}, f32[2352,256]{1,0:T(8,128)}, u32[]{:S(2)}) copy-start(f32[2352,256]{1,0:T(8,128)} %reshape.1096) | copy-start | bytes 7225348
  342.9 7.2 %copy-start.28 = (f32[2352,256]{1,0:T(8,128)S(1)}, f32[2352,256]{1,0:T(8,128)}, u32[]{:S(2)}) copy-start(f32[2352,256]{1,0:T(8,128)} %get-tuple-element.437) | copy-start | bytes 7225348
  358.7 168.3 %reduce-scatter.3.cloned.1.call-start = ((), (), s32[]{:S(2)}) async-start(), calls=%async_computation.4 | async-start | bytes 1327104 | tf_op jit(solution)/shard_map/reduce_scatter | solution.py:197
  439.9 10.5 %copy-start.12 = (bf16[2352,256]{1,0:T(8,128)(2,1)S(1)}, bf16[2352,256]{1,0:T(8,128)(2,1)}, u32[]{:S(2)}) copy-start(bf16[2352,256]{1,0:T(8,128)(2,1)} %multiply_convert_fusion) | copy-start | bytes 3612676
  492.0 2.0 copy-start.24
  492.0 2.0 copy-start.26
  498.8 73.4 %all-to-all-start.1 = ((bf16[8,2,14,14,256]{4,1,3,2,0:T(2,128)(2,1)}), bf16[8,2,14,14,256]{4,1,3,2,0:T(2,128)(2,1)S(1)}, u32[]{:S(2)}, u32[]{:S(2)}) async-start(bf16[8,2,14,14,256]{4,1,3,2,0:T(2,128)(2,1)} %broadcast_select_fusion.1), calls=%async_computation.1 | async-start | bytes 3211264 | tf_op jit(solution)/shard_map/all_to_all | solution.py:192
  502.5 69.0 %all-reduce.7.cloned.1.call-start = ((), (), s32[]{:S(2)}) async-start(), calls=%async_computation.8 | async-start | bytes 589824 | tf_op jit(solution)/shard_map/psum | solution.py:205
  527.0 105.9 %all-gather.3.cloned.1.call-start = ((), (), s32[]{:S(2)}) async-start(), calls=%async_computation.5 | async-start | bytes 1327104 | tf_op jit(solution)/shard_map/all_gather | solution.py:209
  571.6 85.0 %all-gather.5.cloned.1.call-start = ((), (), s32[]{:S(2)}) async-start(), calls=%async_computation.7 | async-start | bytes 1327104 | tf_op jit(solution)/shard_map/all_gather | solution.py:212
  632.9 26.6 %copy-start.1 = (bf16[3,3,256,256]{3,2,1,0:T(8,128)(2,1)S(1)}, bf16[3,3,256,256]{3,2,1,0:T(8,128)(2,1)}, u32[]{:S(2)}) copy-start(bf16[3,3,256,256]{3,2,1,0:T(8,128)(2,1)} %param.53) | copy-start | bytes 3538948
  (5 other events, 8.4 us)
Sparse Core Ops, SparseCore 0:
  358.8 63.7 reduce-scatter.4
  459.0 67.9 reduce-scatter.2
  529.3 42.1 all-reduce.6
  573.6 41.1 all-gather.2
  616.7 39.8 all-gather.4
where the time goes:
time: 678 us; the launch traced here: 666 us
  local copies, waits for them, and re-layouts  311 us (46%)
  other arithmetic  149 us (22%)
  waiting for transfers between devices  120 us (18%)
  matrix products  60.4 us (9%)
  between operations  14.6 us (2%)
  starting transfers between devices  11.4 us (2%)
    scatter-add x18, local copies, waits for them, and re-layouts, refold(): padded.at[:, row_off:row_off + extent, col_off:col_off + extent, :]  178 us
    add x14, other arithmetic, refold(): padded.at[:, row_off:row_off + extent, col_off:col_off + extent, :]  65.3 us
    psum x1, waiting for transfers between devices, on_device(): lax.psum(shares[0].astype(jnp.bfloat16), 'group').astype(jnp.float32)  44.5 us
    unnamed x71, local copies, waits for them, and re-layouts  37 us
    all_to_all x1, waiting for transfers between devices, on_device(): lax.all_to_all(sent_blocks, 'tile', split_axis=0, concat_axis=0, tiled=True)  29.8 us
    concatenate x10, local copies, waits for them, and re-layouts, unfold(): jnp.concatenate(pieces, axis=-1)  25.7 us
    reduce_scatter x1, waiting for transfers between devices, on_device(): lax.psum_scatter(first_raw.astype(jnp.bfloat16), 'tile', scatter_dimensio...  24.4 us
    scatter-add x2, other arithmetic, spread_one_block(): running_sum = running_sum.at[flat_rows + 1].add(upper_terms)  23.8 us
  transfers between devices with their start and end apart: 7, of which 4 were waited for; matrix products, arithmetic and copies ran while one was open for 32% of the time, Pallas kernels for 0%

commit v1 on v0

v1 whole, which is shorter than its diff:
```python
import functools
import math

import jax
import jax.numpy as jnp
from jax import lax
from jax.experimental import pallas as pl
from jax.experimental.pallas import tpu as pltpu
from jax.sharding import PartitionSpec as P

BF = jnp.bfloat16
F32 = jnp.float32
VMEM_BYTES = 60 * 1024 * 1024


def sigmoid(v):
    return jax.nn.sigmoid(v)


def keep_columns(shape, width, extent):
    rows = lax.broadcasted_iota(jnp.int32, shape, 0)
    return (rows % width) < extent


def store_shifted(ref, lead, width, values):
    rows, channels = values.shape
    shifted = (
        pltpu.roll(values, 1, 0),
        values,
        pltpu.roll(values, rows - 1, 0),
    )
    for part in range(3):
        block = shifted[part].astype(BF)
        ref[lead + (pl.ds(width, rows), pl.ds(part * channels, channels))] = block


def conv_taps(ref, lead, width, rows, weight_ref):
    total = None
    for tap in range(3):
        term = jnp.dot(
            ref[lead + (pl.ds(tap * width, rows), slice(None))],
            weight_ref[tap],
            preferred_element_type=F32,
        )
        total = term if total is None else total + term
    return total


def forward_kernel(
    extent, width, group,
    live_ref, low_ref, lw_ref, uw_ref,
    image_ref, mix_ref, w1_ref, w2_ref,
    x3_ref, h3_ref, s1_ref, s2_ref,
    stripe_ref,
):
    slot = pl.program_id(0)
    across = image_ref.shape[1]
    channels = image_ref.shape[2]
    rows = extent * width
    padded = x3_ref.shape[1]

    @pl.when(slot == 0)
    def _():
        stripe_ref[...] = jnp.zeros_like(stripe_ref)

    @pl.when(live_ref[slot] > 0)
    def _():
        for p in range(extent):
            low = low_ref[slot * extent + p]
            lower = image_ref[low].astype(F32) * lw_ref[slot * extent + p]
            upper = image_ref[low + 1].astype(F32) * uw_ref[slot * extent + p]
            stripe_ref[p * across : (p + 1) * across, :] = (lower + upper).astype(BF)
        x3_ref[0, 0:width, :] = jnp.zeros((width, 3 * channels), BF)
        start = width
        part_rows = group * width
        for half in range(stripe_ref.shape[0] // (group * across)):
            mixed = jnp.dot(
                mix_ref[0],
                stripe_ref[half * group * across : (half + 1) * group * across, :],
                preferred_element_type=F32,
            )
            count = min(part_rows, padded - start)
            for shift in range(3):
                x3_ref[0, start : start + count, shift * channels : (shift + 1) * channels] = mixed[
                    shift * part_rows : shift * part_rows + count
                ].astype(BF)
            start += count
        first_pre = conv_taps(x3_ref, (0,), width, rows, w1_ref)
        keep = keep_columns(first_pre.shape, width, extent)
        sigma = sigmoid(first_pre)
        hidden = jnp.where(keep, first_pre * sigma, 0.0)
        s1_ref[0] = jnp.where(keep, sigma * (1.0 + first_pre * (1.0 - sigma)), 0.0)
        h3_ref[0, 0:width, :] = jnp.zeros((width, 3 * channels), BF)
        h3_ref[0, width + rows : padded, :] = jnp.zeros((padded - width - rows, 3 * channels), BF)
        store_shifted(h3_ref, (0,), width, hidden)
        second_pre = conv_taps(h3_ref, (0,), width, rows, w2_ref)
        sigma = sigmoid(second_pre)
        s2_ref[0] = jnp.where(keep, sigma * (1.0 + second_pre * (1.0 - sigma)), 0.0)


def add_weight_grad(acc_ref, source, delta_ref, lead, width):
    rows, channels = source.shape
    flipped = source.T
    for row_off in range(3):
        part = jnp.dot(
            flipped,
            delta_ref[lead + (pl.ds((2 - row_off) * width, rows), slice(None))],
            preferred_element_type=F32,
        )
        for col_off in range(3):
            at = (2 - col_off) * channels
            acc_ref[3 * row_off + col_off] += part[:, at : at + channels]


def backward_kernel(
    extent, width,
    live_ref,
    up_ref, s2_ref, s1_ref, h_ref, x_ref, w2t_ref,
    d1_ref, g1_ref, g2_ref,
    d2_ref, acc1_ref, acc2_ref,
):
    slot = pl.program_id(0)
    rows = extent * width
    padded = d2_ref.shape[0]
    channels = up_ref.shape[2]

    @pl.when(slot == 0)
    def _():
        d2_ref[...] = jnp.zeros_like(d2_ref)
        acc1_ref[...] = jnp.zeros_like(acc1_ref)
        acc2_ref[...] = jnp.zeros_like(acc2_ref)

    @pl.when(live_ref[slot] > 0)
    def _():
        delta = up_ref[0].astype(F32) * s2_ref[0]
        store_shifted(d2_ref, (), width, delta)
        back = conv_taps(d2_ref, (), width, rows, w2t_ref)
        d1_ref[0, 0:width, :] = jnp.zeros((width, 3 * channels), BF)
        d1_ref[0, width + rows : padded, :] = jnp.zeros((padded - width - rows, 3 * channels), BF)
        store_shifted(d1_ref, (0,), width, back * s1_ref[0])
        add_weight_grad(acc2_ref, h_ref[0, width : width + rows, :], d2_ref, (), width)
        add_weight_grad(acc1_ref, x_ref[0, width : width + rows, :], d1_ref, (0,), width)

    @pl.when(slot == pl.num_programs(0) - 1)
    def _():
        g1_ref[...] = acc1_ref[...].astype(BF)
        g2_ref[...] = acc2_ref[...].astype(BF)


def spread_kernel(
    extent, width, group,
    live_ref, low_ref, lw_ref, uw_ref,
    d1_ref, mixt_ref, w1t_ref,
    grad_ref,
    sum_ref,
):
    slot = pl.program_id(0)
    rows = extent * width
    across = grad_ref.shape[1]

    @pl.when(slot == 0)
    def _():
        sum_ref[...] = jnp.zeros_like(sum_ref)

    @pl.when(live_ref[slot] > 0)
    def _():
        back = conv_taps(d1_ref, (0,), width, rows, w1t_ref).astype(BF)
        for first in range(0, extent, group):
            count = min(group, extent - first)
            stripes = jnp.dot(
                mixt_ref[0, 0 : count * across, 0 : count * width],
                back[first * width : (first + count) * width],
                preferred_element_type=F32,
            )
            stripes = stripes.astype(BF).astype(F32)
            for p in range(count):
                at = slot * extent + first + p
                low = low_ref[at]
                stripe = stripes[p * across : (p + 1) * across]
                sum_ref[low] += stripe * lw_ref[at]
                sum_ref[low + 1] += stripe * uw_ref[at]

    @pl.when(slot == pl.num_programs(0) - 1)
    def _():
        grad_ref[...] = sum_ref[...].astype(BF)


def compiler_params():
    return pltpu.CompilerParams(
        dimension_semantics=("arbitrary",), vmem_limit_bytes=VMEM_BYTES
    )


def whole(shape):
    return pl.BlockSpec(shape, lambda *_: (0,) * len(shape))


def by_slot(shape, column=0):
    return pl.BlockSpec((1,) + shape, lambda i, *_: (i, 0, column))


def exchange(value, axis, bit, size):
    return lax.ppermute(value, axis, [(i, i ^ bit) for i in range(size)])


def total_over(values, steps):
    acc = values.astype(F32)
    taken = []
    for axis, bit, size in steps:
        side = (lax.axis_index(axis) // bit) % 2
        half = acc.shape[0] // 2
        keep = lax.dynamic_slice_in_dim(acc, side * half, half, 0)
        send = lax.dynamic_slice_in_dim(acc, (1 - side) * half, half, 0).astype(BF)
        acc = keep + exchange(send, axis, bit, size).astype(F32)
        taken.append((axis, bit, size, side))
    out = acc.astype(BF)
    for axis, bit, size, side in reversed(taken):
        other = exchange(out, axis, bit, size)
        low = jnp.where(side == 0, out, other)
        high = jnp.where(side == 0, other, out)
        out = jnp.concatenate([low, high], axis=0)
    return out


def bits_of(axis, size):
    bit = 1
    while bit < size:
        yield (axis, bit, size)
        bit *= 2


def on_device(features, out_grad, pair_count, sample_grid, first_kernel, second_kernel):
    tiles = lax.axis_size("tile")
    groups = lax.axis_size("group")
    own = lax.axis_index("tile")
    image = features[0]
    height, across, channels = image.shape
    counts = pair_count[0]
    grid = sample_grid[0, 0]
    capacity = grid.shape[1]
    extent = grid.shape[3]
    upstream = out_grad[0]
    regions = upstream.shape[0]
    slots = tiles * capacity
    width = -(-(extent + 1) // 16) * 16
    padded = (extent + 2) * width
    rows = extent * width
    group = max(1, 256 // across)
    stripe_rows = -(-(extent + 1) // group) * group * across
    slot_ids = jnp.arange(capacity, dtype=jnp.int32)

    recv_counts = lax.dynamic_index_in_dim(counts, own, 1, keepdims=False)
    recv_live = (slot_ids[None, :] < recv_counts[:, None]).reshape(-1)
    placed = jnp.maximum(jnp.cumsum(recv_live.astype(jnp.int32), dtype=jnp.int32) - 1, 0)
    wide = jnp.pad(upstream, ((0, 0), (0, 0), (0, width - extent), (0, 0)))
    outgoing = jnp.take(wide.reshape(regions, rows, channels), placed, axis=0)
    outgoing = outgoing.reshape(tiles, capacity, rows, channels)
    up_slots = lax.all_to_all(outgoing, "tile", split_axis=0, concat_axis=0, tiled=True)
    up_slots = up_slots.reshape(slots, rows, channels)

    send_counts = lax.dynamic_index_in_dim(counts, own, 0, keepdims=False)
    live = (slot_ids[None, :] < send_counts[:, None]).astype(jnp.int32).reshape(-1)
    low = grid[..., 0, :].reshape(-1)
    upper = (grid[..., 1, :].astype(F32) / 16.0).reshape(-1)
    lower = 1.0 - upper

    col_low = grid[..., 2, :].reshape(slots, extent)
    col_up = grid[..., 3, :].reshape(slots, extent).astype(F32) / 16.0
    wide_low = jnp.pad(col_low, ((0, 0), (1, width - extent + 1)), constant_values=-8)
    wide_up = jnp.pad(col_up, ((0, 0), (1, width - extent + 1)))
    lows = jnp.stack([wide_low[:, b : b + width] for b in range(3)], axis=1)
    ups = jnp.stack([wide_up[:, b : b + width] for b in range(3)], axis=1)
    places = jnp.arange(across, dtype=jnp.int32)
    cols = jnp.where(places == lows[..., None], 1.0 - ups[..., None], 0.0)
    cols = cols + jnp.where(places == lows[..., None] + 1, ups[..., None], 0.0)
    same = jnp.eye(group, dtype=F32)
    mix = same[None, None, :, None, :, None] * cols[:, :, None, :, None, :]
    mix = mix.astype(BF).reshape(slots, 3 * group * width, group * across)
    centre = cols[:, 1]
    mix_t = same[None, :, None, :, None] * jnp.swapaxes(centre, 1, 2)[:, None, :, None, :]
    mix_t = mix_t.astype(BF).reshape(slots, group * across, group * width)

    w1 = first_kernel.reshape(3, 3 * channels, channels)
    w2 = second_kernel.reshape(3, 3 * channels, channels)

    def turned(kernel):
        return jnp.swapaxes(kernel[::-1, ::-1], 2, 3).reshape(3, 3 * channels, channels)

    wt_shape = (3, 3 * channels, channels)
    map3 = jax.ShapeDtypeStruct((slots, padded, 3 * channels), BF)
    slope = jax.ShapeDtypeStruct((slots, rows, channels), F32)
    x3, h3, s1, s2 = pl.pallas_call(
        functools.partial(forward_kernel, extent, width, group),
        out_shape=(map3, map3, slope, slope),
        grid_spec=pltpu.PrefetchScalarGridSpec(
            num_scalar_prefetch=4,
            grid=(slots,),
            in_specs=[
                whole(image.shape),
                by_slot(mix.shape[1:]),
                whole(wt_shape),
                whole(wt_shape),
            ],
            out_specs=[
                by_slot((padded, 3 * channels)),
                by_slot((padded, 3 * channels)),
                by_slot((rows, channels)),
                by_slot((rows, channels)),
            ],
            scratch_shapes=[pltpu.VMEM((stripe_rows, channels), BF)],
        ),
        compiler_params=compiler_params(),
        name="forward",
    )(live, low, lower, upper, image, mix, w1, w2)

    taps = jax.ShapeDtypeStruct((9, channels, channels), BF)
    d1, g1, g2 = pl.pallas_call(
        functools.partial(backward_kernel, extent, width),
        out_shape=(map3, taps, taps),
        grid_spec=pltpu.PrefetchScalarGridSpec(
            num_scalar_prefetch=1,
            grid=(slots,),
            in_specs=[
                by_slot((rows, channels)),
                by_slot((rows, channels)),
                by_slot((rows, channels)),
                by_slot((padded, channels), 1),
                by_slot((padded, channels), 1),
                whole(wt_shape),
            ],
            out_specs=[
                by_slot((padded, 3 * channels)),
                whole(taps.shape),
                whole(taps.shape),
            ],
            scratch_shapes=[
                pltpu.VMEM((padded, 3 * channels), BF),
                pltpu.VMEM((9, channels, channels), F32),
                pltpu.VMEM((9, channels, channels), F32),
            ],
        ),
        compiler_params=compiler_params(),
        name="backward",
    )(live, up_slots, s2, s1, h3, x3, turned(second_kernel))

    image_grad = pl.pallas_call(
        functools.partial(spread_kernel, extent, width, group),
        out_shape=jax.ShapeDtypeStruct(image.shape, BF),
        grid_spec=pltpu.PrefetchScalarGridSpec(
            num_scalar_prefetch=4,
            grid=(slots,),
            in_specs=[
                by_slot((padded, 3 * channels)),
                by_slot(mix_t.shape[1:]),
                whole(wt_shape),
            ],
            out_specs=whole(image.shape),
            scratch_shapes=[pltpu.VMEM(image.shape, F32)],
        ),
        compiler_params=compiler_params(),
        name="spread",
    )(live, low, lower, upper, d1, mix_t, turned(first_kernel))

    steps = list(bits_of("group", groups)) + list(bits_of("tile", tiles))
    scale = 1.0 / math.sqrt(groups * tiles * regions * extent * extent)
    both = jnp.concatenate([g1, g2], axis=0).reshape(2 * 9 * channels, channels)
    summed = total_over(both, steps).astype(F32) * scale
    summed = summed.reshape(2, 3, 3, channels, channels)
    return (image_grad[None], summed[0], summed[1])


def solution(mesh):
    return jax.shard_map(
        on_device,
        mesh=mesh,
        in_specs=(
            P("group", "tile", None, None),
            P("group", "tile", None, None, None),
            P("group", None, None),
            P("group", "tile", None, None, None, None),
            P(),
            P(),
        ),
        out_specs=(P("group", "tile", None, None), P(), P()),
        check_vma=False,
    )
```

time: 678 us -> 230 us (0.34); the launches traced: 666 us -> 229 us
  local copies, waits for them, and re-layouts: 311 us -> 63.5 us
  other arithmetic: 149 us -> 18.8 us
  Pallas kernels: 0 us -> 71.8 us
  waiting for transfers between devices: 120 us -> 50.1 us
  matrix products: 60.4 us -> 0 us
  between operations: 14.6 us -> 1.01 us
  starting transfers between devices: 11.4 us -> 23.3 us
    scatter-add x18 -> x0, local copies, waits for them, and re-layouts: 178 us -> none  [refold(): padded.at[:, row_off:row_off + extent, col_off:col_off + extent, :]]
    pallas_call x0 -> x3, Pallas kernels: none -> 71.8 us  [the longest x1 29.1 us: on_device(): pl.pallas_call(functools.partial(forward_kernel, extent, width, group), o...]
    add x15 -> x5, other arithmetic: 65.3 us -> 3.71 us  [the longest x4 3.24 us: total_over(): acc = keep + exchange(send, axis, bit, size).astype(F32)]
    dot_general x10 -> x0, matrix products: 60.4 us -> none  [the longest x2 9.96 us: spread_one_block(): jnp.einsum('sqx,spqc->spxc', col_part, grad_part, preferred_element_type=...]
    ppermute x0 -> x10, waiting for transfers between devices: none -> 50.1 us  [exchange(): return lax.ppermute(value, axis, [(i, i ^ bit) for i in range(size)])]
    scatter-add x4 -> x0, other arithmetic: 47.5 us -> none  [the longest x2 23.8 us: spread_one_block(): running_sum = running_sum.at[flat_rows + 1].add(upper_terms)]
    psum x1 -> x0, waiting for transfers between devices: 44.5 us -> none  [on_device(): lax.psum(shares[0].astype(jnp.bfloat16), 'group').astype(jnp.float32)]
    mul x0 -> x10, local copies, waits for them, and re-layouts: none -> 43.1 us  [the longest x4 30.8 us: on_device(): mix = same[None, None, :, None, :, None] * cols[:, :, None, :, None, :]]
  transfers between devices with their start and end apart: 7 -> 11, of which waited for: 4 -> 9; matrix products, arithmetic and copies ran while one was open for 32% -> 27% of each run, Pallas kernels for 0% -> 20%
where the time goes in v1:
time: 230 us; the launch traced here: 229 us
  Pallas kernels  71.8 us (31%)
  local copies, waits for them, and re-layouts  63.5 us (28%)
  waiting for transfers between devices  50.1 us (22%)
  starting transfers between devices  23.3 us (10%)
  other arithmetic  18.8 us (8%)
    ppermute x10, waiting for transfers between devices, exchange(): return lax.ppermute(value, axis, [(i, i ^ bit) for i in range(size)])  50.1 us
    mul x4, local copies, waits for them, and re-layouts, on_device(): mix = same[None, None, :, None, :, None] * cols[:, :, None, :, None, :]  30.8 us
    pallas_call x1, Pallas kernels, on_device(): pl.pallas_call(functools.partial(forward_kernel, extent, width, group), o...  29.1 us
    pallas_call x1, Pallas kernels, on_device(): pl.pallas_call(functools.partial(backward_kernel, extent, width), out_sha...  25.4 us
    pallas_call x1, Pallas kernels, on_device(): pl.pallas_call(functools.partial(spread_kernel, extent, width, group), ou...  17.3 us
    ppermute x10, starting transfers between devices, exchange(): return lax.ppermute(value, axis, [(i, i ^ bit) for i in range(size)])  15.9 us
    mul x6, local copies, waits for them, and re-layouts, on_device(): same[None, :, None, :, None]  12.3 us
    transpose x4, local copies, waits for them, and re-layouts, turned(): jnp.swapaxes(kernel[::-1, ::-1], 2, 3).reshape(3, 3 * channels, channels)  7.81 us
  transfers between devices with their start and end apart: 11, of which 9 were waited for; matrix products, arithmetic and copies ran while one was open for 27% of the time, Pallas kernels for 20%

profile of v1, /device:TPU:0, one launch (start us, length us, event | category | flops | bytes accessed | tf_op | source)
XLA Modules:
  0.0 228.6 jit_solution(11525163982167074500)
XLA Ops:
  5.7 7.4 %all-to-all-start = ((bf16[8,2,224,256]{3,2,1,0:T(8,128)(2,1)}), bf16[8,2,224,256]{3,2,1,0:T(8,128)(2,1)S(1)}, u32[]{:S(2)}, u32[]{:S(2)}) async-start(bf16[8,2,224,256]{3,2,1,0:T(8,128)(2,1)} %broadcast_select_fusion), calls=%async_computation | async-start | bytes 3670016 | tf_op jit(solution)/shard_map/all_to_all | solution.py:258
  14.6 11.5 %mul.79 = f32[16,3,8,16,8,32]{5,4,3,2,1,0:T(8,128)} broadcast(f32[16,3,16,32]{3,2,1,0:T(8,128)S(1)} %copy.15), dimensions={0,1,3,5} | broadcast | bytes 6389760 | tf_op jit(solution)/shard_map/mul | solution.py:277
  26.2 17.9 %mul.80 = f32[16,384,256]{2,1,0:T(8,128)} reshape(f32[16,3,8,16,8,32]{5,4,3,2,1,0:T(8,128)} %mul.79) | data formatting | bytes 12582912 | tf_op jit(solution)/shard_map/mul | solution.py:277
  48.4 1.5 copy.16
  50.5 5.1 %multiply_convert_fusion.mix_ref = bf16[16,384,256]{2,1,0:T(8,128)(2,1)} fusion(f32[16,384,256]{2,1,0:T(8,128)} %mul.80, f32[384,256]{1,0:T(8,128)S(1)} %copy-done.6), kind=kLoop, calls=%fused_computation.1 | loop fusion | flops 3145728 | bytes 9830400 | tf_op jit(solution)/shard_map/convert_element_type | solution.py:278
  55.7 29.1 %forward.1 = (bf16[16,256,768]{2,1,0:T(8,128)(2,1)}, bf16[16,256,768]{2,1,0:T(8,128)(2,1)}, f32[16,224,256]{2,1,0:T(8,128)}, f32[16,224,256]{2,1,0:T(8,128)}) custom-call(s32[16]{0:T(128)} %reshape.196.live_ref, s32[224]{0:T(256)} %reshape_squeeze.7.low_ref, f32[224]{0:T(256)} %broadcast_subtract_fusion.1.lw_ref, f32[224]{0:T(256)} %copy-done.8, ...), custom_call_target="tpu_custom_call" | custom-call | tf_op jit(solution)/shard_map/forward/pallas_call | solution.py:292
  85.9 25.4 %backward.1 = (bf16[16,256,768]{2,1,0:T(8,128)(2,1)}, bf16[9,256,256]{2,1,0:T(8,128)(2,1)}, bf16[9,256,256]{2,1,0:T(8,128)(2,1)}) custom-call(s32[16]{0:T(128)} %reshape.196.live_ref, bf16[16,224,256]{2,1,0:T(8,128)(2,1)} %bitcast.53, f32[16,224,256]{2,1,0:T(8,128)} %get-tuple-element.10.s2_ref, f32[16,224,256]{2,1,0:T(8,128)} %get-tuple-element.11.s1_ref, ...), custom_call_target="tpu_custom_call" | custom-call | tf_op jit(solution)/shard_map/backward/pallas_call | solution.py:317
  111.4 1.8 pad_maximum_fusion
  113.8 2.1 copy-done.2
  116.1 2.8 %collective-permute-done = bf16[2304,256]{1,0:T(8,128)(2,1)S(1)} collective-permute-done((bf16[2304,256]{1,0:T(8,128)(2,1)S(1)}, bf16[2304,256]{1,0:T(8,128)(2,1)S(1)}, u32[]{:S(2)}, u32[]{:S(2)}) %collective-permute-start) | collective-permute-done | bytes 1179680 | tf_op jit(solution)/shard_map/ppermute | solution.py:203
  118.9 2.0 convert_add_fusion
  121.1 15.4 %collective-permute-done.1 = bf16[1152,256]{1,0:T(8,128)(2,1)} collective-permute-done((bf16[1152,256]{1,0:T(8,128)(2,1)S(1)}, bf16[1152,256]{1,0:T(8,128)(2,1)}, u32[]{:S(2)}, u32[]{:S(2)}) %collective-permute-start.1) | collective-permute-done | bytes 589856 | tf_op jit(solution)/shard_map/ppermute | solution.py:203
  137.7 2.2 collective-permute-start.2
  139.9 6.7 %collective-permute-done.2 = bf16[576,256]{1,0:T(8,128)(2,1)S(1)} collective-permute-done((bf16[576,256]{1,0:T(8,128)(2,1)S(1)}, bf16[576,256]{1,0:T(8,128)(2,1)S(1)}, u32[]{:S(2)}, u32[]{:S(2)}) %collective-permute-start.2) | collective-permute-done | bytes 294944 | tf_op jit(solution)/shard_map/ppermute | solution.py:203
  148.2 3.8 %collective-permute-done.3 = bf16[288,256]{1,0:T(8,128)(2,1)S(1)} collective-permute-done((bf16[288,256]{1,0:T(8,128)(2,1)S(1)}, bf16[288,256]{1,0:T(8,128)(2,1)S(1)}, u32[]{:S(2)}, u32[]{:S(2)}) %collective-permute-start.3) | collective-permute-done | bytes 147488 | tf_op jit(solution)/shard_map/ppermute | solution.py:203
  152.0 2.7 %collective-permute-start.4 = (bf16[144,256]{1,0:T(8,128)(2,1)S(1)}, bf16[144,256]{1,0:T(8,128)(2,1)S(1)}, u32[]{:S(2)}, u32[]{:S(2)}) collective-permute-start(bf16[144,256]{1,0:T(8,128)(2,1)S(1)} %dynamic-slice_convert_fusion.4), channel_id=1, source_target_pairs={{0,16},{4,20},{8,24},{12,28},{16,0},{20,4},{24,8},{28,12},{1,17},{... | collective-permute-start | bytes 221192 | tf_op jit(solution)/shard_map/ppermute | solution.py:203
  154.8 2.6 %collective-permute-done.4 = bf16[144,256]{1,0:T(8,128)(2,1)S(1)} collective-permute-done((bf16[144,256]{1,0:T(8,128)(2,1)S(1)}, bf16[144,256]{1,0:T(8,128)(2,1)S(1)}, u32[]{:S(2)}, u32[]{:S(2)}) %collective-permute-start.4) | collective-permute-done | bytes 73760 | tf_op jit(solution)/shard_map/ppermute | solution.py:203
  157.4 3.1 %collective-permute-start.5 = (bf16[144,256]{1,0:T(8,128)(2,1)S(1)}, bf16[144,256]{1,0:T(8,128)(2,1)S(1)}, u32[]{:S(2)}, u32[]{:S(2)}) collective-permute-start(bf16[144,256]{1,0:T(8,128)(2,1)S(1)} %add_convert_fusion), channel_id=1, source_target_pairs={{0,16},{4,20},{8,24},{12,28},{16,0},{20,4},{24,8},{28,12},{1,17},{... | collective-permute-start | bytes 221192 | tf_op jit(solution)/shard_map/ppermute | solution.py:203
  160.5 2.4 %collective-permute-done.5 = bf16[144,256]{1,0:T(8,128)(2,1)S(1)} collective-permute-done((bf16[144,256]{1,0:T(8,128)(2,1)S(1)}, bf16[144,256]{1,0:T(8,128)(2,1)S(1)}, u32[]{:S(2)}, u32[]{:S(2)}) %collective-permute-start.5) | collective-permute-done | bytes 73760 | tf_op jit(solution)/shard_map/ppermute | solution.py:203
  162.9 2.9 %collective-permute-start.6 = (bf16[288,256]{1,0:T(8,128)(2,1)S(1)}, bf16[288,256]{1,0:T(8,128)(2,1)S(1)}, u32[]{:S(2)}, u32[]{:S(2)}) collective-permute-start(bf16[288,256]{1,0:T(8,128)(2,1)S(1)} %pad_maximum_fusion.4), channel_id=1, source_target_pairs={{0,8},{4,12},{8,0},{12,4},{16,24},{20,28},{24,16},{28,20},{1,9},{5... | collective-permute-start | bytes 442376 | tf_op jit(solution)/shard_map/ppermute | solution.py:203
  165.7 3.1 %collective-permute-done.6 = bf16[288,256]{1,0:T(8,128)(2,1)S(1)} collective-permute-done((bf16[288,256]{1,0:T(8,128)(2,1)S(1)}, bf16[288,256]{1,0:T(8,128)(2,1)S(1)}, u32[]{:S(2)}, u32[]{:S(2)}) %collective-permute-start.6) | collective-permute-done | bytes 147488 | tf_op jit(solution)/shard_map/ppermute | solution.py:203
  170.5 5.3 %collective-permute-done.7 = bf16[576,256]{1,0:T(8,128)(2,1)S(1)} collective-permute-done((bf16[576,256]{1,0:T(8,128)(2,1)S(1)}, bf16[576,256]{1,0:T(8,128)(2,1)S(1)}, u32[]{:S(2)}, u32[]{:S(2)}) %collective-permute-start.7) | collective-permute-done | bytes 294944 | tf_op jit(solution)/shard_map/ppermute | solution.py:203
  175.9 1.9 collective-permute-start.8
  177.8 8.1 %collective-permute-done.8 = bf16[1152,256]{1,0:T(8,128)(2,1)S(1)} collective-permute-done((bf16[1152,256]{1,0:T(8,128)(2,1)S(1)}, bf16[1152,256]{1,0:T(8,128)(2,1)S(1)}, u32[]{:S(2)}, u32[]{:S(2)}) %collective-permute-start.8) | collective-permute-done | bytes 589856 | tf_op jit(solution)/shard_map/ppermute | solution.py:203
  188.1 4.3 %mul.85 = f32[16,8,32,8,16]{2,1,4,3,0:T(8,128)} broadcast(f32[16,32,16]{1,2,0:T(8,128)S(1)} %slice_bitcast_fusion), dimensions={0,2,4} | broadcast | bytes 2129920 | tf_op jit(solution)/shard_map/mul | solution.py:280
  192.4 5.8 %mul.86 = f32[16,256,128]{1,2,0:T(8,128)S(1)} reshape(f32[16,8,32,8,16]{2,1,4,3,0:T(8,128)} %mul.85) | data formatting | bytes 4194304 | tf_op jit(solution)/shard_map/mul | solution.py:280
  198.2 1.8 copy.18
  200.4 2.5 %reverse_bitcast_fusion = bf16[3,3,256,256]{2,3,1,0:T(8,128)(2,1)} fusion(bf16[3,3,256,256]{3,2,1,0:T(8,128)(2,1)} %param.10), kind=kLoop, calls=%fused_computation.12 | loop fusion | bytes 2359296 | tf_op jit(solution)/shard_map/transpose | solution.py:287
  203.0 2.4 %copy.19 = bf16[3,3,256,256]{3,2,1,0:T(8,128)(2,1)} copy(bf16[3,3,256,256]{2,3,1,0:T(8,128)(2,1)} %reverse_bitcast_fusion) | data formatting | bytes 2359296 | tf_op jit(solution)/shard_map/transpose | solution.py:287
  206.5 17.3 %spread.1 = bf16[64,32,256]{2,1,0:T(8,128)(2,1)} custom-call(s32[16]{0:T(128)} %reshape.196.live_ref, s32[224]{0:T(256)} %reshape_squeeze.7.low_ref, f32[224]{0:T(256)} %broadcast_subtract_fusion.1.lw_ref, f32[224]{0:T(256)} %copy-done.8, bf16[16,256,768]{2,1,0:T(8,128)(2,1)} %get-tuple-element.14.d1_ref, ...), custom_call_target="tpu_custom_call" | custom-call | tf_op jit(solution)/shard_map/spread/pallas_call | solution.py:346
  223.9 1.8 broadcast_select_fusion.2
  226.1 2.5 %fusion.8 = (f32[2304,256]{1,0:T(8,128)}, f32[2304,256]{1,0:T(8,128)}) fusion(f32[4608,256]{1,0:T(8,128)S(1)} %convert_multiply_fusion), kind=kLoop, calls=%fused_computation.67 | loop fusion | bytes 9437184 | tf_op jit(solution)/shard_map/slice | solution.py:369
  (78 shorter events, 22.4 us)
Async XLA Ops:
  0.6 0.7 copy-start
  5.7 7.4 %copy-start.7 = (s32[1,1,8,2,4,14]{5,4,3,2,1,0:T(4,128)S(1)}, s32[1,1,8,2,4,14]{5,4,3,2,1,0:T(4,128)}, u32[]{:S(2)}) copy-start(s32[1,1,8,2,4,14]{5,4,3,2,1,0:T(4,128)} %param.9) | copy-start | bytes 10756
  5.7 79.0 %all-to-all-start = ((bf16[8,2,224,256]{3,2,1,0:T(8,128)(2,1)}), bf16[8,2,224,256]{3,2,1,0:T(8,128)(2,1)S(1)}, u32[]{:S(2)}, u32[]{:S(2)}) async-start(bf16[8,2,224,256]{3,2,1,0:T(8,128)(2,1)} %broadcast_select_fusion), calls=%async_computation | async-start | bytes 3670016 | tf_op jit(solution)/shard_map/all_to_all | solution.py:258
  13.9 0.7 copy-start.5
  46.3 3.6 %copy-start.8 = (f32[224]{0:T(256)}, f32[224]{0:T(256)S(1)}, u32[]{:S(2)}) copy-start(f32[224]{0:T(256)S(1)} %div.40.uw_ref) | copy-start | bytes 2692
  47.0 3.5 %copy-start.6 = (f32[384,256]{1,0:T(8,128)S(1)}, f32[384,256]{1,0:T(8,128)}, u32[]{:S(2)}) copy-start(f32[384,256]{1,0:T(8,128)} %mul.77) | copy-start | bytes 1179652
  84.7 1.2 copy-start.4
  113.7 2.1 copy-start.2
  116.0 2.9 %collective-permute-start = (bf16[2304,256]{1,0:T(8,128)(2,1)S(1)}, bf16[2304,256]{1,0:T(8,128)(2,1)S(1)}, u32[]{:S(2)}, u32[]{:S(2)}) collective-permute-start(bf16[2304,256]{1,0:T(8,128)(2,1)S(1)} %dynamic-slice_convert_fusion), channel_id=1, source_target_pairs={{0,1},{1,0},{2,3},{3,2},{4,5},{5,4},{6,7},{7,6},{8,9},{9,8},{10,11... | collective-permute-start | bytes 3538952 | tf_op jit(solution)/shard_map/ppermute | solution.py:203
  120.9 15.5 %collective-permute-start.1 = (bf16[1152,256]{1,0:T(8,128)(2,1)S(1)}, bf16[1152,256]{1,0:T(8,128)(2,1)}, u32[]{:S(2)}, u32[]{:S(2)}) collective-permute-start(bf16[1152,256]{1,0:T(8,128)(2,1)S(1)} %dynamic-slice_convert_fusion.1), channel_id=1, source_target_pairs={{0,2},{1,3},{2,0},{3,1},{4,6},{5,7},{6,4},{7,5},{8,10},{9,11},{10,... | collective-permute-start | bytes 1769480 | tf_op jit(solution)/shard_map/ppermute | solution.py:203
  137.7 8.9 %collective-permute-start.2 = (bf16[576,256]{1,0:T(8,128)(2,1)S(1)}, bf16[576,256]{1,0:T(8,128)(2,1)S(1)}, u32[]{:S(2)}, u32[]{:S(2)}) collective-permute-start(bf16[576,256]{1,0:T(8,128)(2,1)S(1)} %dynamic-slice_convert_fusion.2), channel_id=1, source_target_pairs={{0,4},{4,0},{8,12},{12,8},{16,20},{20,16},{24,28},{28,24},{1,5},{5... | collective-permute-start | bytes 884744 | tf_op jit(solution)/shard_map/ppermute | solution.py:203
  146.8 5.2 %collective-permute-start.3 = (bf16[288,256]{1,0:T(8,128)(2,1)S(1)}, bf16[288,256]{1,0:T(8,128)(2,1)S(1)}, u32[]{:S(2)}, u32[]{:S(2)}) collective-permute-start(bf16[288,256]{1,0:T(8,128)(2,1)S(1)} %dynamic-slice_convert_fusion.3), channel_id=1, source_target_pairs={{0,8},{4,12},{8,0},{12,4},{16,24},{20,28},{24,16},{28,20},{1,9},{5... | collective-permute-start | bytes 442376 | tf_op jit(solution)/shard_map/ppermute | solution.py:203
  152.0 5.3 %collective-permute-start.4 = (bf16[144,256]{1,0:T(8,128)(2,1)S(1)}, bf16[144,256]{1,0:T(8,128)(2,1)S(1)}, u32[]{:S(2)}, u32[]{:S(2)}) collective-permute-start(bf16[144,256]{1,0:T(8,128)(2,1)S(1)} %dynamic-slice_convert_fusion.4), channel_id=1, source_target_pairs={{0,16},{4,20},{8,24},{12,28},{16,0},{20,4},{24,8},{28,12},{1,17},{... | collective-permute-start | bytes 221192 | tf_op jit(solution)/shard_map/ppermute | solution.py:203
  157.4 5.5 %collective-permute-start.5 = (bf16[144,256]{1,0:T(8,128)(2,1)S(1)}, bf16[144,256]{1,0:T(8,128)(2,1)S(1)}, u32[]{:S(2)}, u32[]{:S(2)}) collective-permute-start(bf16[144,256]{1,0:T(8,128)(2,1)S(1)} %add_convert_fusion), channel_id=1, source_target_pairs={{0,16},{4,20},{8,24},{12,28},{16,0},{20,4},{24,8},{28,12},{1,17},{... | collective-permute-start | bytes 221192 | tf_op jit(solution)/shard_map/ppermute | solution.py:203
  162.9 6.0 %collective-permute-start.6 = (bf16[288,256]{1,0:T(8,128)(2,1)S(1)}, bf16[288,256]{1,0:T(8,128)(2,1)S(1)}, u32[]{:S(2)}, u32[]{:S(2)}) collective-permute-start(bf16[288,256]{1,0:T(8,128)(2,1)S(1)} %pad_maximum_fusion.4), channel_id=1, source_target_pairs={{0,8},{4,12},{8,0},{12,4},{16,24},{20,28},{24,16},{28,20},{1,9},{5... | collective-permute-start | bytes 442376 | tf_op jit(solution)/shard_map/ppermute | solution.py:203
  169.0 6.8 %collective-permute-start.7 = (bf16[576,256]{1,0:T(8,128)(2,1)S(1)}, bf16[576,256]{1,0:T(8,128)(2,1)S(1)}, u32[]{:S(2)}, u32[]{:S(2)}) collective-permute-start(bf16[576,256]{1,0:T(8,128)(2,1)S(1)} %pad_maximum_fusion.3), channel_id=1, source_target_pairs={{0,4},{4,0},{8,12},{12,8},{16,20},{20,16},{24,28},{28,24},{1,5},{5... | collective-permute-start | bytes 884744 | tf_op jit(solution)/shard_map/ppermute | solution.py:203
  175.9 9.9 %collective-permute-start.8 = (bf16[1152,256]{1,0:T(8,128)(2,1)S(1)}, bf16[1152,256]{1,0:T(8,128)(2,1)S(1)}, u32[]{:S(2)}, u32[]{:S(2)}) collective-permute-start(bf16[1152,256]{1,0:T(8,128)(2,1)S(1)} %pad_maximum_fusion.2), channel_id=1, source_target_pairs={{0,2},{1,3},{2,0},{3,1},{4,6},{5,7},{6,4},{7,5},{8,10},{9,11},{10,... | collective-permute-start | bytes 1769480 | tf_op jit(solution)/shard_map/ppermute | solution.py:203
  187.2 36.7 %collective-permute-start.9 = (bf16[2304,256]{1,0:T(8,128)(2,1)}, bf16[2304,256]{1,0:T(8,128)(2,1)}, u32[]{:S(2)}, u32[]{:S(2)}) collective-permute-start(bf16[2304,256]{1,0:T(8,128)(2,1)} %pad_maximum_fusion.1), channel_id=1, source_target_pairs={{0,1},{1,0},{2,3},{3,2},{4,5},{5,4},{6,7},{7,6},{8,9},{9,8},{10,11... | collective-permute-start | bytes 3538952 | tf_op jit(solution)/shard_map/ppermute | solution.py:203
  200.4 4.9 %copy-start.3 = (f32[16,256,128]{2,1,0:T(8,128)S(1)}, f32[16,256,128]{2,1,0:T(8,128)}, u32[]{:S(2)}) copy-start(f32[16,256,128]{2,1,0:T(8,128)} %copy.18) | copy-start | bytes 6291460
  226.1 2.5 %copy-start.1 = (s32[1,8,8]{2,1,0:T(8,128)S(1)}, s32[1,8,8]{2,1,0:T(8,128)}, u32[]{:S(2)}) copy-start(s32[1,8,8]{2,1,0:T(8,128)} %param.8) | copy-start | bytes 772

commit v2 on v1

v2 whole, which is shorter than its diff:
```python
import functools
import math

import jax
import jax.numpy as jnp
from jax import lax
from jax.experimental import pallas as pl
from jax.experimental.pallas import tpu as pltpu
from jax.sharding import PartitionSpec as P

BF = jnp.bfloat16
F32 = jnp.float32
VMEM_BYTES = 60 * 1024 * 1024
FAR = 1.0e6
AXES = ("tile", "group")


def iota(shape, dim):
    return lax.broadcasted_iota(jnp.int32, shape, dim)


def shifted_copies(values):
    rows = values.shape[0]
    return (pltpu.roll(values, 1, 0), values, pltpu.roll(values, rows - 1, 0))


def store_shifted(ref, slot, start, values):
    rows, channels = values.shape
    for part, block in enumerate(shifted_copies(values)):
        ref[slot, start : start + rows, part * channels : (part + 1) * channels] = block.astype(BF)


def conv_taps(ref, start, width, rows, weight_ref):
    count = ref.shape[0]
    total = None
    for tap in range(3):
        at = start + tap * width
        left = ref[:, at : at + rows, :].reshape(count * rows, ref.shape[2])
        term = jnp.dot(left, weight_ref[tap], preferred_element_type=F32)
        total = term if total is None else total + term
    return total


def hat(base_ref, index_ref, start, step):
    place = start + step * index_ref[...]
    return jnp.maximum(1.0 - jnp.abs(base_ref[...] - place) * 0.0625, 0.0).astype(BF)


def row_place(meta_ref, slot, p):
    at = meta_ref[4 * slot] + meta_ref[4 * slot + 1] * p
    return at // 16, (at % 16).astype(F32) * 0.0625


def forward_kernel(
    extent, width, group, capacity,
    live_ref, meta_ref,
    image_ref, w1_ref, w2_ref,
    xt_ref, ht_ref, s1_ref, s2_ref, w1t_ref, w2t_ref,
    stripe_ref, x3_ref, h3_ref, base_ref, index_ref,
):
    step = pl.program_id(0)
    across = image_ref.shape[1]
    channels = image_ref.shape[2]
    rows = extent * width
    padded = x3_ref.shape[1]
    part_rows = group * width

    @pl.when(step == 0)
    def _():
        stripe_ref[...] = jnp.zeros_like(stripe_ref)
        x3_ref[...] = jnp.zeros_like(x3_ref)
        h3_ref[...] = jnp.zeros_like(h3_ref)
        shape = base_ref.shape
        row, lane = iota(shape, 0), iota(shape, 1)
        index = row % width + row // part_rows - 1
        fits = (lane // across == (row % part_rows) // width) & (index >= 0) & (index < extent)
        fits = fits & (row % width < extent)
        base_ref[...] = jnp.where(fits, (16 * (lane % across)).astype(F32), FAR)
        index_ref[...] = index.astype(F32)
        for source, target in ((w1_ref, w1t_ref), (w2_ref, w2t_ref)):
            for a in range(3):
                for b in range(3):
                    tap = source[2 - a, (2 - b) * channels : (3 - b) * channels, :]
                    target[a, b * channels : (b + 1) * channels, :] = tap.T

    busy = live_ref[step * capacity]
    for g in range(1, capacity):
        busy = busy + live_ref[step * capacity + g]

    @pl.when(busy > 0)
    def _():
        for g in range(capacity):
            slot = step * capacity + g
            alive = live_ref[slot].astype(F32)
            for p in range(extent):
                low, share = row_place(meta_ref, slot, p)
                lower = image_ref[low].astype(F32) * ((1.0 - share) * alive)
                upper = image_ref[low + 1].astype(F32) * (share * alive)
                stripe_ref[g, p * across : (p + 1) * across, :] = (lower + upper).astype(BF)
            mix = hat(
                base_ref, index_ref,
                meta_ref[4 * slot + 2].astype(F32), meta_ref[4 * slot + 3].astype(F32),
            )
            start = width
            for half in range(stripe_ref.shape[1] // (group * across)):
                mixed = jnp.dot(
                    mix,
                    stripe_ref[g, half * group * across : (half + 1) * group * across, :],
                    preferred_element_type=F32,
                )
                count = min(part_rows, padded - start)
                for b in range(3):
                    block = mixed[b * part_rows : b * part_rows + count]
                    x3_ref[g, start : start + count, b * channels : (b + 1) * channels] = (
                        block.astype(BF)
                    )
                start += count
        pre = conv_taps(x3_ref, 0, width, rows, w1_ref)
        keep = (iota((rows, channels), 0) % width) < extent
        for g in range(capacity):
            value = pre[g * rows : (g + 1) * rows]
            sigma = jax.nn.sigmoid(value)
            s1_ref[g] = jnp.where(keep, sigma * (1.0 + value * (1.0 - sigma)), 0.0)
            store_shifted(h3_ref, g, width, jnp.where(keep, value * sigma, 0.0))
            xt_ref[g] = x3_ref[g].T
        pre = conv_taps(h3_ref, 0, width, rows, w2_ref)
        for g in range(capacity):
            value = pre[g * rows : (g + 1) * rows]
            sigma = jax.nn.sigmoid(value)
            s2_ref[g] = jnp.where(keep, sigma * (1.0 + value * (1.0 - sigma)), 0.0)
            ht_ref[g] = h3_ref[g].T


def add_weight_grad(acc_ref, source_ref, delta_ref, width):
    count, deep, padded = source_ref.shape
    channels = deep // 3
    left = jnp.concatenate([source_ref[g] for g in range(count)], axis=1)
    for a in range(3):
        at = (2 - a) * width
        right = delta_ref[:, at : at + padded, channels : 2 * channels]
        part = jnp.dot(left, right.reshape(count * padded, channels), preferred_element_type=F32)
        acc_ref[a * deep : (a + 1) * deep, :] += part


def backward_kernel(
    extent, width, first_step, parts, carried, last, blocks,
    live_ref, order_ref, *refs,
):
    up_refs, refs = refs[:parts], refs[parts:]
    s2_ref, s1_ref, ht_ref, xt_ref, w2t_ref, *refs = refs
    if carried:
        in1_ref, in2_ref, *refs = refs
    d1_ref, *refs = refs
    if last:
        sums_ref, *refs = refs
    else:
        out1_ref, out2_ref, *refs = refs
    up_ref, d2_ref, d1s_ref, acc1_ref, acc2_ref = refs
    step = pl.program_id(0)
    rows = extent * width
    capacity = up_ref.shape[0]
    channels = up_ref.shape[2]

    @pl.when(step == 0)
    def _():
        up_ref[...] = jnp.zeros_like(up_ref)
        d2_ref[...] = jnp.zeros_like(d2_ref)
        d1s_ref[...] = jnp.zeros_like(d1s_ref)
        if carried:
            acc1_ref[...] = in1_ref[...]
            acc2_ref[...] = in2_ref[...]
        else:
            acc1_ref[...] = jnp.zeros_like(acc1_ref)
            acc2_ref[...] = jnp.zeros_like(acc2_ref)

    busy = live_ref[(first_step + step) * capacity]
    for g in range(1, capacity):
        busy = busy + live_ref[(first_step + step) * capacity + g]

    for part in range(parts):
        @pl.when((busy > 0) & (step == part))
        def _():
            for g in range(capacity):
                for i in range(extent):
                    up_ref[g, i * width : i * width + extent, :] = up_refs[part][g, i]

    @pl.when(busy > 0)
    def _():
        for g in range(capacity):
            store_shifted(d2_ref, g, 2 * width, up_ref[g].astype(F32) * s2_ref[g])
        back = conv_taps(d2_ref, width, width, rows, w2t_ref)
        for g in range(capacity):
            store_shifted(d1s_ref, g, 2 * width, back[g * rows : (g + 1) * rows] * s1_ref[g])
        add_weight_grad(acc2_ref, ht_ref, d2_ref, width)
        add_weight_grad(acc1_ref, xt_ref, d1s_ref, width)
        d1_ref[...] = d1s_ref[:, width : width + d1_ref.shape[1], :]

    @pl.when(step == pl.num_programs(0) - 1)
    def _():
        if last:
            size = acc1_ref.shape[0] // blocks
            for k in range(blocks):
                at = pl.multiple_of((order_ref[0] ^ k) * size, size)
                for j, (zero, one) in enumerate(
                    ((acc1_ref, acc2_ref), (acc2_ref, acc1_ref))
                ):
                    @pl.when(order_ref[1] == 0)
                    def _():
                        sums_ref[j, k * size : (k + 1) * size, :] = zero[pl.ds(at, size)].astype(BF)

                    @pl.when(order_ref[1] != 0)
                    def _():
                        sums_ref[j, k * size : (k + 1) * size, :] = one[pl.ds(at, size)].astype(BF)
        else:
            out1_ref[...] = acc1_ref[...]
            out2_ref[...] = acc2_ref[...]


def spread_kernel(
    extent, width, group, capacity,
    live_ref, meta_ref,
    d1_ref, w1t_ref,
    grad_ref,
    sum_ref, base_ref, index_ref,
):
    step = pl.program_id(0)
    rows = extent * width
    across = grad_ref.shape[1]

    @pl.when(step == 0)
    def _():
        sum_ref[...] = jnp.zeros_like(sum_ref)
        shape = base_ref.shape
        row, lane = iota(shape, 0), iota(shape, 1)
        index = lane % width
        fits = (row // across == lane // width) & (index < extent)
        base_ref[...] = jnp.where(fits, (16 * (row % across)).astype(F32), FAR)
        index_ref[...] = index.astype(F32)

    busy = live_ref[step * capacity]
    for g in range(1, capacity):
        busy = busy + live_ref[step * capacity + g]

    @pl.when(busy > 0)
    def _():
        back = conv_taps(d1_ref, 0, width, rows, w1t_ref).astype(BF)
        for g in range(capacity):
            slot = step * capacity + g
            alive = live_ref[slot].astype(F32)
            mix = hat(
                base_ref, index_ref,
                meta_ref[4 * slot + 2].astype(F32), meta_ref[4 * slot + 3].astype(F32),
            )
            for first in range(0, extent, group):
                count = min(group, extent - first)
                at = g * rows + first * width
                stripes = jnp.dot(
                    mix[0 : count * across, 0 : count * width],
                    back[at : at + count * width],
                    preferred_element_type=F32,
                ).astype(BF).astype(F32)
                for p in range(count):
                    low, share = row_place(meta_ref, slot, first + p)
                    stripe = stripes[p * across : (p + 1) * across]
                    sum_ref[low] += stripe * ((1.0 - share) * alive)
                    sum_ref[low + 1] += stripe * (share * alive)

    @pl.when(step == pl.num_programs(0) - 1)
    def _():
        grad_ref[...] = sum_ref[...].astype(BF)


def finish_kernel(scale, inner, order_ref, own_ref, other_ref, first_ref, second_ref):
    size = own_ref.shape[0] // inner
    low = order_ref[0] % inner

    def place(source, target):
        for k in range(inner):
            at = pl.multiple_of((low ^ k) * size, size)
            target[k * size : (k + 1) * size, :] = source[pl.ds(at, size)].astype(F32) * scale

    @pl.when(order_ref[1] == 0)
    def _():
        place(own_ref, first_ref)
        place(other_ref, second_ref)

    @pl.when(order_ref[1] != 0)
    def _():
        place(other_ref, first_ref)
        place(own_ref, second_ref)


def compiler_params():
    return pltpu.CompilerParams(
        dimension_semantics=("arbitrary",), vmem_limit_bytes=VMEM_BYTES
    )


def whole(shape):
    return pl.BlockSpec(shape, lambda *_: (0,) * len(shape))


def stepped(shape, base=0):
    return pl.BlockSpec(shape, lambda i, *_: (i + base,) + (0,) * (len(shape) - 1))


def partner(value, mask, total):
    return lax.ppermute(value, AXES, [(i, i ^ mask) for i in range(total)])


def masks_of(bits):
    found = [0]
    for bit in bits:
        found = found + [m | bit for m in found]
    return found


def bits_below(size):
    return [1 << n for n in range(size.bit_length() - 1)]


def plan_stages(tiles, groups):
    group_bits = bits_below(groups)
    tile_bits = [bit * groups for bit in bits_below(tiles)]
    bits = group_bits + tile_bits
    head, rest = bits[:1], bits[1:]
    stages = []
    if len(group_bits) > 1 and tile_bits:
        joined = [tile_bits[0], group_bits[-1]]
        stages.append(joined)
        rest = [bit for bit in rest if bit not in joined]
    stages.extend([bit] for bit in rest)
    return head, stages


def reduce_stage(value, bits, total):
    masks = masks_of(bits)
    size = value.shape[0] // len(masks)
    got = [
        partner(value[k * size : (k + 1) * size], masks[k], total) for k in range(1, len(masks))
    ]
    acc = value[:size].astype(F32)
    for piece in got:
        acc = acc + piece.astype(F32)
    return acc.astype(BF)


def gather_stage(value, bits, total):
    masks = masks_of(bits)
    return jnp.concatenate([value] + [partner(value, m, total) for m in masks[1:]], axis=0)


def on_device(features, out_grad, pair_count, sample_grid, first_kernel, second_kernel):
    tiles = lax.axis_size("tile")
    groups = lax.axis_size("group")
    total = tiles * groups
    own = lax.axis_index("tile")
    image = features[0]
    height, across, channels = image.shape
    counts = pair_count[0]
    grid = sample_grid[0, 0]
    capacity = grid.shape[1]
    extent = grid.shape[3]
    upstream = out_grad[0]
    regions = upstream.shape[0]
    slots = tiles * capacity
    width = -(-(extent + 1) // 16) * 16
    padded = (extent + 2) * width
    rows = extent * width
    deep = 3 * channels
    group = max(1, 256 // across)
    stripe_rows = -(-(extent + 1) // group) * group * across
    slot_ids = jnp.arange(capacity, dtype=jnp.int32)
    peers = jnp.arange(tiles, dtype=jnp.int32) ^ own

    recv_counts = lax.dynamic_index_in_dim(counts, own, 1, keepdims=False)
    before = jnp.sum(
        jnp.where(jnp.arange(tiles)[None, :] < peers[:, None], recv_counts[None, :], 0),
        axis=1, dtype=jnp.int32,
    )
    source = jnp.minimum(before[:, None] + slot_ids[None, :], regions - 1).reshape(-1)
    outgoing = upstream.at[source].get(mode="promise_in_bounds")
    outgoing = outgoing.reshape((tiles, capacity) + upstream.shape[1:])
    arrived = [outgoing[0]]
    for k in range(1, tiles):
        arrived.append(
            lax.ppermute(outgoing[k], "tile", [(i, i ^ k) for i in range(tiles)])
        )

    send_counts = lax.dynamic_index_in_dim(counts, own, 0, keepdims=False)
    live = (slot_ids[None, :] < send_counts[peers][:, None]).astype(jnp.int32).reshape(-1)
    mine = grid[peers]
    starts = 16 * mine[:, :, 0::2, 0] + mine[:, :, 1::2, 0]
    nexts = 16 * mine[:, :, 0::2, 1] + mine[:, :, 1::2, 1]
    meta = jnp.stack([starts, nexts - starts], axis=-1).reshape(-1).astype(jnp.int32)

    w1 = first_kernel.reshape(3, deep, channels)
    w2 = second_kernel.reshape(3, deep, channels)
    turned = jax.ShapeDtypeStruct(w1.shape, BF)
    flipped = jax.ShapeDtypeStruct((slots, deep, padded), BF)
    slope = jax.ShapeDtypeStruct((slots, rows, channels), F32)
    map_spec = (capacity, padded, deep)
    flip_spec = (capacity, deep, padded)
    slope_spec = (capacity, rows, channels)
    mix_rows = 3 * group * width
    xt, ht, s1, s2, w1t, w2t = pl.pallas_call(
        functools.partial(forward_kernel, extent, width, group, capacity),
        out_shape=(flipped, flipped, slope, slope, turned, turned),
        grid_spec=pltpu.PrefetchScalarGridSpec(
            num_scalar_prefetch=2,
            grid=(tiles,),
            in_specs=[whole(image.shape), whole(w1.shape), whole(w2.shape)],
            out_specs=[
                stepped(flip_spec), stepped(flip_spec), stepped(slope_spec), stepped(slope_spec),
                whole(w1.shape), whole(w2.shape),
            ],
            scratch_shapes=[
                pltpu.VMEM((capacity, stripe_rows, channels), BF),
                pltpu.VMEM(map_spec, BF),
                pltpu.VMEM(map_spec, BF),
                pltpu.VMEM((mix_rows, group * across), F32),
                pltpu.VMEM((mix_rows, group * across), F32),
            ],
        ),
        compiler_params=compiler_params(),
        name="forward",
    )(live, meta, image, w1, w2)

    head, stages = plan_stages(tiles, groups)
    blocks = 1
    for bits in stages:
        blocks *= 2 ** len(bits)
    relative = (9 * channels) % (16 * blocks) == 0 and blocks >= 4
    flat = lax.axis_index("tile") * groups + lax.axis_index("group")
    if relative:
        order = jnp.int32(0)
        for bits in stages:
            for bit in reversed(bits):
                order = 2 * order + (flat // bit) % 2
        order = jnp.stack([order, (flat // head[0]) % 2]).astype(jnp.int32)
    else:
        blocks = 1
        order = jnp.zeros((2,), jnp.int32)

    def backward(first, parts, carried, last):
        acc = jax.ShapeDtypeStruct((9 * channels, channels), F32)
        d1_shape = jax.ShapeDtypeStruct((parts * capacity, padded, deep), BF)
        if last:
            sums = jax.ShapeDtypeStruct((2, 9 * channels, channels), BF)
            outs, out_specs = (sums,), [whole(sums.shape)]
        else:
            outs, out_specs = (acc, acc), [whole(acc.shape)] * 2
        ups = arrived[first : first + parts]
        return pl.pallas_call(
            functools.partial(
                backward_kernel, extent, width, first, parts, bool(carried), last, blocks
            ),
            out_shape=(d1_shape,) + outs,
            grid_spec=pltpu.PrefetchScalarGridSpec(
                num_scalar_prefetch=2,
                grid=(parts,),
                in_specs=[whole(up.shape) for up in ups]
                + [
                    stepped(slope_spec, first), stepped(slope_spec, first),
                    stepped(flip_spec, first), stepped(flip_spec, first),
                    whole(w2t.shape),
                ]
                + [whole(acc.shape) for _ in carried],
                out_specs=[stepped(map_spec)] + out_specs,
                scratch_shapes=[
                    pltpu.VMEM(slope_spec, BF),
                    pltpu.VMEM((capacity, padded + 2 * width, deep), BF),
                    pltpu.VMEM((capacity, padded + 2 * width, deep), BF),
                    pltpu.VMEM(acc.shape, F32),
                    pltpu.VMEM(acc.shape, F32),
                ],
            ),
            compiler_params=compiler_params(),
            name="backward",
        )(live, order, *ups, s2, s1, ht, xt, w2t, *carried)

    late = max(1, tiles // 4)
    early_d1, acc1, acc2 = backward(0, tiles - late, (), False)
    late_d1, sums = backward(tiles - late, late, (acc1, acc2), True)

    d1 = jnp.concatenate([early_d1, late_d1], axis=0)

    def spread(d1):
        return pl.pallas_call(
            functools.partial(spread_kernel, extent, width, group, capacity),
            out_shape=jax.ShapeDtypeStruct(image.shape, BF),
            grid_spec=pltpu.PrefetchScalarGridSpec(
                num_scalar_prefetch=2,
                grid=(tiles,),
                in_specs=[stepped(map_spec), whole(w1t.shape)],
                out_specs=whole(image.shape),
                scratch_shapes=[
                    pltpu.VMEM(image.shape, F32),
                    pltpu.VMEM((group * across, group * width), F32),
                    pltpu.VMEM((group * across, group * width), F32),
                ],
            ),
            compiler_params=compiler_params(),
            name="spread",
        )(live, meta, d1, w1t)

    scale = 1.0 / math.sqrt(total * regions * extent * extent)
    if not relative:
        image_grad = spread(d1)
        summed = lax.psum(sums, AXES).astype(F32) * scale
        first_grad, second_grad = summed[0], summed[1]
    else:
        got = partner(sums[1], head[0], total)
        value = (sums[0].astype(F32) + got.astype(F32)).astype(BF)
        value, d1 = lax.optimization_barrier((value, d1))
        image_grad = spread(d1)
        value = reduce_stage(value, stages[0], total)
        value, image_grad = lax.optimization_barrier((value, image_grad))
        for bits in stages[1:]:
            value = reduce_stage(value, bits, total)
        for bits in reversed(stages):
            value = gather_stage(value, bits, total)
        other = partner(value, head[0], total)
        inner = 4
        outer = blocks // inner
        piece = (9 * channels // outer, channels)
        full = jax.ShapeDtypeStruct((9 * channels, channels), F32)
        first_grad, second_grad = pl.pallas_call(
            functools.partial(finish_kernel, scale, inner),
            out_shape=(full, full),
            grid_spec=pltpu.PrefetchScalarGridSpec(
                num_scalar_prefetch=1,
                grid=(outer,),
                in_specs=[
                    pl.BlockSpec(piece, lambda i, order: (i ^ (order[0] // inner), 0))
                ] * 2,
                out_specs=[pl.BlockSpec(piece, lambda i, order: (i, 0))] * 2,
            ),
            compiler_params=compiler_params(),
            name="finish",
        )(order, value, other)
    shape = (3, 3, channels, channels)
    return (image_grad[None], first_grad.reshape(shape), second_grad.reshape(shape))


def solution(mesh):
    return jax.shard_map(
        on_device,
        mesh=mesh,
        in_specs=(
            P("group", "tile", None, None),
            P("group", "tile", None, None, None),
            P("group", None, None),
            P("group", "tile", None, None, None, None),
            P(),
            P(),
        ),
        out_specs=(P("group", "tile", None, None), P(), P()),
        check_vma=False,
    )
```

time: 230 us -> 164 us (0.71)
  local copies, waits for them, and re-layouts: 63.5 us -> 12.4 us
  other arithmetic: 18.8 us -> 7.3 us
  waiting for transfers between devices: 50.1 us -> 41.5 us
  Pallas kernels: 71.8 us -> 77.2 us
    mul x10 -> x0, local copies, waits for them, and re-layouts: 43.1 us -> none  [the longest x4 30.8 us: on_device(): mix = same[None, None, :, None, :, None] * cols[:, :, None, :, None, :]]
    transpose x5 -> x0, local copies, waits for them, and re-layouts: 8.72 us -> none  [the longest x4 7.81 us: turned(): jnp.swapaxes(kernel[::-1, ::-1], 2, 3).reshape(3, 3 * channels, channels)]
    ppermute x10 -> x19, waiting for transfers between devices: 50.1 us -> 41.5 us  [the longest x12 30.6 us: partner(): return lax.ppermute(value, AXES, [(i, i ^ mask) for i in range(total)])]
    ppermute x10 -> x19, starting transfers between devices: 15.9 us -> 24.5 us  [the longest x7 13.9 us: on_device(): lax.ppermute(outgoing[k], 'tile', [(i, i ^ k) for i in range(tiles)])]
    all_to_all x1 -> x0, starting transfers between devices: 7.41 us -> none  [on_device(): lax.all_to_all(outgoing, 'tile', split_axis=0, concat_axis=0, tiled=True)]
    convert_element_type x7 -> x4, other arithmetic: 7.05 us -> 0.56 us  [the longest x1 0.3 us: on_device(): value = (sums[0].astype(F32) + got.astype(F32)).astype(BF)]
    pallas_call x3 -> x5, Pallas kernels: 71.8 us -> 77.2 us  [the longest x2 30.4 us: backward(): pl.pallas_call(functools.partial(backward_kernel, extent, width, first, p...]
    add x5 -> x0, other arithmetic: 3.71 us -> none  [the longest x4 3.24 us: total_over(): acc = keep + exchange(send, axis, bit, size).astype(F32)]
  transfers between devices with their start and end apart: 11 -> 19, of which waited for: 9 -> 11; matrix products, arithmetic and copies ran while one was open for 27% -> 7% of each run, Pallas kernels for 20% -> 37%
where the time goes in v2:
time: 164 us
  Pallas kernels  77.2 us (47%)
  waiting for transfers between devices  41.5 us (25%)
  starting transfers between devices  24.5 us (15%)
  local copies, waits for them, and re-layouts  12.4 us (8%)
  other arithmetic  7.3 us (4%)
    ppermute x12, waiting for transfers between devices, partner(): return lax.ppermute(value, AXES, [(i, i ^ mask) for i in range(total)])  30.6 us
    pallas_call x2, Pallas kernels, backward(): pl.pallas_call(functools.partial(backward_kernel, extent, width, first, p...  30.4 us
    pallas_call x1, Pallas kernels, on_device(): pl.pallas_call(functools.partial(forward_kernel, extent, width, group, ca...  29.3 us
    ppermute x7, starting transfers between devices, on_device(): lax.ppermute(outgoing[k], 'tile', [(i, i ^ k) for i in range(tiles)])  13.9 us
    pallas_call x1, Pallas kernels, spread(): pl.pallas_call(functools.partial(spread_kernel, extent, width, group, cap...  12.5 us
    ppermute x7, waiting for transfers between devices, on_device(): lax.ppermute(outgoing[k], 'tile', [(i, i ^ k) for i in range(tiles)])  10.9 us
    ppermute x12, starting transfers between devices, partner(): return lax.ppermute(value, AXES, [(i, i ^ mask) for i in range(total)])  10.6 us
    concatenate x1, other arithmetic, on_device(): d1 = jnp.concatenate([early_d1, late_d1], axis=0)  5.66 us
  transfers between devices with their start and end apart: 19, of which 11 were waited for; matrix products, arithmetic and copies ran while one was open for 7% of the time, Pallas kernels for 37%

profile of v2, /device:TPU:0, one launch (start us, length us, event | category | flops | bytes accessed | tf_op | source)
XLA Modules:
  0.0 163.8 jit_solution(9173677503280022808)
XLA Ops:
  0.7 1.0 dynamic-slice_reduce_fusion
  2.7 1.1 fusion.4
  3.8 5.0 %collective-permute-start.6 = (bf16[2,14,14,256]{3,2,1,0:T(8,128)(2,1)}, bf16[2,14,14,256]{3,2,1,0:T(8,128)(2,1)S(1)}, u32[]{:S(2)}, u32[]{:S(2)}) collective-permute-start(bf16[2,14,14,256]{3,2,1,0:T(8,128)(2,1)} %get-tuple-element.41), channel_id=1, source_target_pairs={{0,20},{4,16},{8,28},{12,24},{16,4},{20,0},{24,12},{28,8},{1,21},{... | collective-permute-start | bytes 602120 | tf_op jit(solution)/shard_map/ppermute | solution.py:387
  9.2 1.5 collective-permute-start.4
  10.8 1.8 %collective-permute-start.2 = (bf16[2,14,14,256]{3,2,1,0:T(8,128)(2,1)}, bf16[2,14,14,256]{3,2,1,0:T(8,128)(2,1)S(1)}, u32[]{:S(2)}, u32[]{:S(2)}) collective-permute-start(bf16[2,14,14,256]{3,2,1,0:T(8,128)(2,1)} %get-tuple-element.45), channel_id=1, source_target_pairs={{0,4},{4,0},{8,12},{12,8},{16,20},{20,16},{24,28},{28,24},{1,5},{5... | collective-permute-start | bytes 602120 | tf_op jit(solution)/shard_map/ppermute | solution.py:387
  13.9 0.7 slice.78
  15.0 0.7 slice.79
  17.1 8.3 %collective-permute-done.6.refs_5_ = bf16[2,14,14,256]{3,2,1,0:T(8,128)(2,1)S(1)} collective-permute-done((bf16[2,14,14,256]{3,2,1,0:T(8,128)(2,1)}, bf16[2,14,14,256]{3,2,1,0:T(8,128)(2,1)S(1)}, u32[]{:S(2)}, u32[]{:S(2)}) %collective-permute-start.6) | collective-permute-done | bytes 200736 | tf_op jit(solution)/shard_map/ppermute | solution.py:387
  25.4 3.7 %collective-permute-start.1 = (bf16[2,14,14,256]{3,2,1,0:T(8,128)(2,1)S(1)}, bf16[2,14,14,256]{3,2,1,0:T(8,128)(2,1)S(1)}, u32[]{:S(2)}, u32[]{:S(2)}) collective-permute-start(bf16[2,14,14,256]{3,2,1,0:T(8,128)(2,1)S(1)} %get-tuple-element.47), channel_id=1, source_target_pairs={{0,28},{4,24},{8,20},{12,16},{16,12},{20,8},{24,4},{28,0},{1,29},{... | collective-permute-start | bytes 602120 | tf_op jit(solution)/shard_map/ppermute | solution.py:387
  29.1 2.6 %collective-permute-done.5.refs_4_ = bf16[2,14,14,256]{3,2,1,0:T(8,128)(2,1)S(1)} collective-permute-done((bf16[2,14,14,256]{3,2,1,0:T(8,128)(2,1)}, bf16[2,14,14,256]{3,2,1,0:T(8,128)(2,1)S(1)}, u32[]{:S(2)}, u32[]{:S(2)}) %collective-permute-start.5) | collective-permute-done | bytes 200736 | tf_op jit(solution)/shard_map/ppermute | solution.py:387
  31.7 1.4 collective-permute-start
  33.9 29.3 %forward.1 = (bf16[16,768,256]{2,1,0:T(8,128)(2,1)}, bf16[16,768,256]{2,1,0:T(8,128)(2,1)}, f32[16,224,256]{2,1,0:T(8,128)}, f32[16,224,256]{2,1,0:T(8,128)}, bf...) custom-call(s32[16]{0:T(128)} %reshape.112.live_ref, s32[64]{0:T(128)} %reshape.107.meta_ref, ...), custom_call_target="tpu_custom_call" | custom-call | tf_op jit(solution)/shard_map/forward/pallas_call | solution.py:406
  64.6 19.0 %backward.2 = (bf16[12,256,768]{2,1,0:T(8,128)(2,1)}, f32[2304,256]{1,0:T(8,128)}, f32[2304,256]{1,0:T(8,128)}) custom-call(s32[16]{0:T(128)} %reshape.112.live_ref, s32[2]{0:T(128)} %pad_add_fusion.1.order_ref, bf16[2,14,14,256]{3,2,1,0:T(8,128)(2,1)} %get-tuple-element.46.refs_0_, bf16[2,14,14,256]{3,2,1,0:T(8,128)(2,1)} %copy-done.10, ...), custom_call_target="tpu_custom_call" | custom-call | tf_op jit(solution)/shard_map/backward/pallas_call | solution.py:454
  84.4 11.4 %backward.3 = (bf16[4,256,768]{2,1,0:T(8,128)(2,1)}, bf16[2,2304,256]{2,1,0:T(8,128)(2,1)}) custom-call(s32[16]{0:T(128)} %reshape.112.live_ref, s32[2]{0:T(128)} %pad_add_fusion.1.order_ref, bf16[2,14,14,256]{3,2,1,0:T(8,128)(2,1)} %copy-done.12, bf16[2,14,14,256]{3,2,1,0:T(8,128)(2,1)} %copy-done.11, f32[16,224,256]{2,1,0:T(8,128)} %get-tuple-element.20.refs_6_.refs_2_, ...), custom_call_target="tpu_custom_call" | custom-call | tf_op jit(solution)/shard_map/backward/pallas_call | solution.py:454
  95.8 1.5 slice_bitcast_fusion
  97.5 5.7 %pad_maximum_fusion.d1_ref = bf16[16,256,768]{2,1,0:T(8,128)(2,1)} fusion(bf16[4,256,768]{2,1,0:T(8,128)(2,1)S(1)} %copy-done.3, bf16[12,256,768]{2,1,0:T(8,128)(2,1)} %get-tuple-element.28), kind=kLoop, calls=%fused_computation.3 | loop fusion | flops 3145728 | bytes 12582912 | tf_op jit(solution)/shard_map/concatenate | solution.py:486
  104.2 2.5 %collective-permute-start.10 = (bf16[576,256]{1,0:T(8,128)(2,1)S(1)}, bf16[576,256]{1,0:T(8,128)(2,1)S(1)}, u32[]{:S(2)}, u32[]{:S(2)}) collective-permute-start(bf16[576,256]{1,0:T(8,128)(2,1)S(1)} %get-tuple-element.50), channel_id=1, source_target_pairs={{0,6},{1,7},{2,4},{3,5},{4,2},{5,3},{6,0},{7,1},{8,14},{9,15},{10,... | collective-permute-start | bytes 884744 | tf_op jit(solution)/shard_map/ppermute | solution.py:308
  107.1 12.5 %spread.1 = bf16[64,32,256]{2,1,0:T(8,128)(2,1)} custom-call(s32[16]{0:T(128)} %reshape.112.live_ref, s32[64]{0:T(128)} %reshape.107.meta_ref, bf16[16,256,768]{2,1,0:T(8,128)(2,1)} %pad_maximum_fusion.d1_ref, bf16[3,768,256]{2,1,0:T(8,128)(2,1)} %get-tuple-element.32.w1t_ref), custom_call_target="tpu_custom_call" | custom-call | tf_op jit(solution)/shard_map/spread/pallas_call | solution.py:489
  120.2 1.4 collective-permute-done.9
  121.8 5.1 %collective-permute-done.11 = bf16[288,256]{1,0:T(8,128)(2,1)S(1)} collective-permute-done((bf16[288,256]{1,0:T(8,128)(2,1)S(1)}, bf16[288,256]{1,0:T(8,128)(2,1)S(1)}, u32[]{:S(2)}, u32[]{:S(2)}) %collective-permute-start.11) | collective-permute-done | bytes 147488 | tf_op jit(solution)/shard_map/ppermute | solution.py:308
  127.0 1.1 collective-permute-start.12
  128.1 4.6 %collective-permute-done.12 = bf16[144,256]{1,0:T(8,128)(2,1)S(1)} collective-permute-done((bf16[144,256]{1,0:T(8,128)(2,1)S(1)}, bf16[144,256]{1,0:T(8,128)(2,1)S(1)}, u32[]{:S(2)}, u32[]{:S(2)}) %collective-permute-start.12) | collective-permute-done | bytes 73760 | tf_op jit(solution)/shard_map/ppermute | solution.py:308
  132.7 0.8 collective-permute-start.13
  133.4 4.9 %collective-permute-done.13 = bf16[144,256]{1,0:T(8,128)(2,1)S(1)} collective-permute-done((bf16[144,256]{1,0:T(8,128)(2,1)S(1)}, bf16[144,256]{1,0:T(8,128)(2,1)S(1)}, u32[]{:S(2)}, u32[]{:S(2)}) %collective-permute-start.13) | collective-permute-done | bytes 73760 | tf_op jit(solution)/shard_map/ppermute | solution.py:308
  138.4 1.5 collective-permute-start.14
  139.8 3.7 %collective-permute-done.14 = bf16[288,256]{1,0:T(8,128)(2,1)S(1)} collective-permute-done((bf16[288,256]{1,0:T(8,128)(2,1)S(1)}, bf16[288,256]{1,0:T(8,128)(2,1)S(1)}, u32[]{:S(2)}, u32[]{:S(2)}) %collective-permute-start.14) | collective-permute-done | bytes 147488 | tf_op jit(solution)/shard_map/ppermute | solution.py:308
  144.5 2.6 %collective-permute-start.17 = (bf16[576,256]{1,0:T(8,128)(2,1)S(1)}, bf16[576,256]{1,0:T(8,128)(2,1)S(1)}, u32[]{:S(2)}, u32[]{:S(2)}) collective-permute-start(bf16[576,256]{1,0:T(8,128)(2,1)S(1)} %pad_maximum_fusion.1), channel_id=1, source_target_pairs={{0,6},{1,7},{2,4},{3,5},{4,2},{5,3},{6,0},{7,1},{8,14},{9,15},{10,... | collective-permute-start | bytes 884744 | tf_op jit(solution)/shard_map/ppermute | solution.py:308
  147.2 4.1 %collective-permute-done.15 = bf16[576,256]{1,0:T(8,128)(2,1)S(1)} collective-permute-done((bf16[576,256]{1,0:T(8,128)(2,1)S(1)}, bf16[576,256]{1,0:T(8,128)(2,1)S(1)}, u32[]{:S(2)}, u32[]{:S(2)}) %collective-permute-start.15) | collective-permute-done | bytes 294944 | tf_op jit(solution)/shard_map/ppermute | solution.py:308
  151.2 3.4 %collective-permute-done.16 = bf16[576,256]{1,0:T(8,128)(2,1)S(1)} collective-permute-done((bf16[576,256]{1,0:T(8,128)(2,1)S(1)}, bf16[576,256]{1,0:T(8,128)(2,1)S(1)}, u32[]{:S(2)}, u32[]{:S(2)}) %collective-permute-start.16) | collective-permute-done | bytes 294944 | tf_op jit(solution)/shard_map/ppermute | solution.py:308
  154.8 2.8 %collective-permute-done.18.other_ref = bf16[2304,256]{1,0:T(8,128)(2,1)S(1)} collective-permute-done((bf16[2304,256]{1,0:T(8,128)(2,1)S(1)}, bf16[2304,256]{1,0:T(8,128)(2,1)S(1)}, u32[]{:S(2)}, u32[]{:S(2)}) %collective-permute-start.18) | collective-permute-done | bytes 1179680 | tf_op jit(solution)/shard_map/ppermute | solution.py:308
  157.7 1.0 copy-done.5
  158.7 5.0 %finish.1 = (f32[2304,256]{1,0:T(8,128)}, f32[2304,256]{1,0:T(8,128)}) custom-call(s32[2]{0:T(128)} %pad_add_fusion.1.order_ref, bf16[2304,256]{1,0:T(8,128)(2,1)} %copy-done.4, bf16[2304,256]{1,0:T(8,128)(2,1)} %copy-done.5), custom_call_target="tpu_custom_call" | custom-call | tf_op jit(solution)/shard_map/finish/pallas_call | solution.py:528
  (78 shorter events, 11.3 us)
Async XLA Ops:
  0.6 1.4 copy-start
  2.7 10.6 %copy-start.13 = (s32[1,1,8,2,4,14]{5,4,3,2,1,0:T(4,128)S(1)}, s32[1,1,8,2,4,14]{5,4,3,2,1,0:T(4,128)}, u32[]{:S(2)}) copy-start(s32[1,1,8,2,4,14]{5,4,3,2,1,0:T(4,128)} %param.9) | copy-start | bytes 10756
  3.8 21.6 %collective-permute-start.6 = (bf16[2,14,14,256]{3,2,1,0:T(8,128)(2,1)}, bf16[2,14,14,256]{3,2,1,0:T(8,128)(2,1)S(1)}, u32[]{:S(2)}, u32[]{:S(2)}) collective-permute-start(bf16[2,14,14,256]{3,2,1,0:T(8,128)(2,1)} %get-tuple-element.41), channel_id=1, source_target_pairs={{0,20},{4,16},{8,28},{12,24},{16,4},{20,0},{24,12},{28,8},{1,21},{... | collective-permute-start | bytes 602120 | tf_op jit(solution)/shard_map/ppermute | solution.py:387
  8.8 22.9 %collective-permute-start.5 = (bf16[2,14,14,256]{3,2,1,0:T(8,128)(2,1)}, bf16[2,14,14,256]{3,2,1,0:T(8,128)(2,1)S(1)}, u32[]{:S(2)}, u32[]{:S(2)}) collective-permute-start(bf16[2,14,14,256]{3,2,1,0:T(8,128)(2,1)} %get-tuple-element.42), channel_id=1, source_target_pairs={{0,16},{4,20},{8,24},{12,28},{16,0},{20,4},{24,8},{28,12},{1,17},{... | collective-permute-start | bytes 602120 | tf_op jit(solution)/shard_map/ppermute | solution.py:387
  9.2 54.6 %collective-permute-start.4 = (bf16[2,14,14,256]{3,2,1,0:T(8,128)(2,1)}, bf16[2,14,14,256]{3,2,1,0:T(8,128)(2,1)S(1)}, u32[]{:S(2)}, u32[]{:S(2)}) collective-permute-start(bf16[2,14,14,256]{3,2,1,0:T(8,128)(2,1)} %get-tuple-element.43), channel_id=1, source_target_pairs={{0,12},{4,8},{8,4},{12,0},{16,28},{20,24},{24,20},{28,16},{1,13},{... | collective-permute-start | bytes 602120 | tf_op jit(solution)/shard_map/ppermute | solution.py:387
  10.7 53.1 %collective-permute-start.3 = (bf16[2,14,14,256]{3,2,1,0:T(8,128)(2,1)}, bf16[2,14,14,256]{3,2,1,0:T(8,128)(2,1)S(1)}, u32[]{:S(2)}, u32[]{:S(2)}) collective-permute-start(bf16[2,14,14,256]{3,2,1,0:T(8,128)(2,1)} %get-tuple-element.44), channel_id=1, source_target_pairs={{0,8},{4,12},{8,0},{12,4},{16,24},{20,28},{24,16},{28,20},{1,9},{5... | collective-permute-start | bytes 602120 | tf_op jit(solution)/shard_map/ppermute | solution.py:387
  10.8 52.9 %collective-permute-start.2 = (bf16[2,14,14,256]{3,2,1,0:T(8,128)(2,1)}, bf16[2,14,14,256]{3,2,1,0:T(8,128)(2,1)S(1)}, u32[]{:S(2)}, u32[]{:S(2)}) collective-permute-start(bf16[2,14,14,256]{3,2,1,0:T(8,128)(2,1)} %get-tuple-element.45), channel_id=1, source_target_pairs={{0,4},{4,0},{8,12},{12,8},{16,20},{20,16},{24,28},{28,24},{1,5},{5... | collective-permute-start | bytes 602120 | tf_op jit(solution)/shard_map/ppermute | solution.py:387
  25.4 37.7 %copy-start.6 = (bf16[2,14,14,256]{3,2,1,0:T(8,128)(2,1)}, bf16[2,14,14,256]{3,2,1,0:T(8,128)(2,1)S(1)}, u32[]{:S(2)}) copy-start(bf16[2,14,14,256]{3,2,1,0:T(8,128)(2,1)S(1)} %collective-permute-done.6.refs_5_) | copy-start | bytes 602116
  25.4 58.2 %collective-permute-start.1 = (bf16[2,14,14,256]{3,2,1,0:T(8,128)(2,1)S(1)}, bf16[2,14,14,256]{3,2,1,0:T(8,128)(2,1)S(1)}, u32[]{:S(2)}, u32[]{:S(2)}) collective-permute-start(bf16[2,14,14,256]{3,2,1,0:T(8,128)(2,1)S(1)} %get-tuple-element.47), channel_id=1, source_target_pairs={{0,28},{4,24},{8,20},{12,16},{16,12},{20,8},{24,4},{28,0},{1,29},{... | collective-permute-start | bytes 602120 | tf_op jit(solution)/shard_map/ppermute | solution.py:387
  31.7 31.4 %copy-start.7 = (bf16[2,14,14,256]{3,2,1,0:T(8,128)(2,1)}, bf16[2,14,14,256]{3,2,1,0:T(8,128)(2,1)S(1)}, u32[]{:S(2)}) copy-start(bf16[2,14,14,256]{3,2,1,0:T(8,128)(2,1)S(1)} %collective-permute-done.5.refs_4_) | copy-start | bytes 602116
  31.7 51.9 %collective-permute-start = (bf16[2,14,14,256]{3,2,1,0:T(8,128)(2,1)S(1)}, bf16[2,14,14,256]{3,2,1,0:T(8,128)(2,1)S(1)}, u32[]{:S(2)}, u32[]{:S(2)}) collective-permute-start(bf16[2,14,14,256]{3,2,1,0:T(8,128)(2,1)S(1)} %get-tuple-element.48), channel_id=1, source_target_pairs={{0,24},{4,28},{8,16},{12,20},{16,8},{20,12},{24,0},{28,4},{1,25},{... | collective-permute-start | bytes 602120 | tf_op jit(solution)/shard_map/ppermute | solution.py:387
  63.8 0.8 copy-start.9
  63.8 0.8 copy-start.10
  83.6 0.7 copy-start.11
  83.6 0.7 copy-start.12
  95.8 1.8 %copy-start.3 = (bf16[4,256,768]{2,1,0:T(8,128)(2,1)S(1)}, bf16[4,256,768]{2,1,0:T(8,128)(2,1)}, u32[]{:S(2)}) copy-start(bf16[4,256,768]{2,1,0:T(8,128)(2,1)} %get-tuple-element.29) | copy-start | bytes 4718596
  97.2 6.0 %collective-permute-start.7 = (bf16[2304,256]{1,0:T(8,128)(2,1)S(1)}, bf16[2304,256]{1,0:T(8,128)(2,1)S(1)}, u32[]{:S(2)}, u32[]{:S(2)}) collective-permute-start(bf16[2304,256]{1,0:T(8,128)(2,1)S(1)} %slice_bitcast_fusion), channel_id=1, source_target_pairs={{0,1},{1,0},{2,3},{3,2},{4,5},{5,4},{6,7},{7,6},{8,9},{9,8},{10,11... | collective-permute-start | bytes 3538952 | tf_op jit(solution)/shard_map/ppermute | solution.py:308
  97.5 5.7 %copy-start.2 = (bf16[2,2304,256]{2,1,0:T(8,128)(2,1)S(1)}, bf16[2,2304,256]{2,1,0:T(8,128)(2,1)}, u32[]{:S(2)}) copy-start(bf16[2,2304,256]{2,1,0:T(8,128)(2,1)} %get-tuple-element.27) | copy-start | bytes 7077892
  103.6 16.1 %collective-permute-start.8 = (bf16[576,256]{1,0:T(8,128)(2,1)S(1)}, bf16[576,256]{1,0:T(8,128)(2,1)S(1)}, u32[]{:S(2)}, u32[]{:S(2)}) collective-permute-start(bf16[576,256]{1,0:T(8,128)(2,1)S(1)} %get-tuple-element.49), channel_id=1, source_target_pairs={{0,4},{1,5},{2,6},{3,7},{4,0},{5,1},{6,2},{7,3},{8,12},{9,13},{10,... | collective-permute-start | bytes 884744 | tf_op jit(solution)/shard_map/ppermute | solution.py:308
  104.2 16.1 %collective-permute-start.10 = (bf16[576,256]{1,0:T(8,128)(2,1)S(1)}, bf16[576,256]{1,0:T(8,128)(2,1)S(1)}, u32[]{:S(2)}, u32[]{:S(2)}) collective-permute-start(bf16[576,256]{1,0:T(8,128)(2,1)S(1)} %get-tuple-element.50), channel_id=1, source_target_pairs={{0,6},{1,7},{2,4},{3,5},{4,2},{5,3},{6,0},{7,1},{8,14},{9,15},{10,... | collective-permute-start | bytes 884744 | tf_op jit(solution)/shard_map/ppermute | solution.py:308
  106.6 15.0 %collective-permute-start.9 = (bf16[576,256]{1,0:T(8,128)(2,1)S(1)}, bf16[576,256]{1,0:T(8,128)(2,1)S(1)}, u32[]{:S(2)}, u32[]{:S(2)}) collective-permute-start(bf16[576,256]{1,0:T(8,128)(2,1)S(1)} %get-tuple-element.51), channel_id=1, source_target_pairs={{0,2},{1,3},{2,0},{3,1},{4,6},{5,7},{6,4},{7,5},{8,10},{9,11},{10,... | collective-permute-start | bytes 884744 | tf_op jit(solution)/shard_map/ppermute | solution.py:308
  121.7 5.2 %collective-permute-start.11 = (bf16[288,256]{1,0:T(8,128)(2,1)S(1)}, bf16[288,256]{1,0:T(8,128)(2,1)S(1)}, u32[]{:S(2)}, u32[]{:S(2)}) collective-permute-start(bf16[288,256]{1,0:T(8,128)(2,1)S(1)} %slice.93), channel_id=1, source_target_pairs={{0,8},{1,9},{2,10},{3,11},{4,12},{5,13},{6,14},{7,15},{8,0},{9,1},... | collective-permute-start | bytes 442376 | tf_op jit(solution)/shard_map/ppermute | solution.py:308
  127.0 5.6 %collective-permute-start.12 = (bf16[144,256]{1,0:T(8,128)(2,1)S(1)}, bf16[144,256]{1,0:T(8,128)(2,1)S(1)}, u32[]{:S(2)}, u32[]{:S(2)}) collective-permute-start(bf16[144,256]{1,0:T(8,128)(2,1)S(1)} %slice.111), channel_id=1, source_target_pairs={{0,16},{1,17},{2,18},{3,19},{4,20},{5,21},{6,22},{7,23},{8,24},{9,... | collective-permute-start | bytes 221192 | tf_op jit(solution)/shard_map/ppermute | solution.py:308
  132.7 5.7 %collective-permute-start.13 = (bf16[144,256]{1,0:T(8,128)(2,1)S(1)}, bf16[144,256]{1,0:T(8,128)(2,1)S(1)}, u32[]{:S(2)}, u32[]{:S(2)}) collective-permute-start(bf16[144,256]{1,0:T(8,128)(2,1)S(1)} %get-tuple-element.38), channel_id=1, source_target_pairs={{0,16},{1,17},{2,18},{3,19},{4,20},{5,21},{6,22},{7,23},{8,24},{9,... | collective-permute-start | bytes 221192 | tf_op jit(solution)/shard_map/ppermute | solution.py:308
  138.4 5.2 %collective-permute-start.14 = (bf16[288,256]{1,0:T(8,128)(2,1)S(1)}, bf16[288,256]{1,0:T(8,128)(2,1)S(1)}, u32[]{:S(2)}, u32[]{:S(2)}) collective-permute-start(bf16[288,256]{1,0:T(8,128)(2,1)S(1)} %pad_maximum_fusion.2), channel_id=1, source_target_pairs={{0,8},{1,9},{2,10},{3,11},{4,12},{5,13},{6,14},{7,15},{8,0},{9,1},... | collective-permute-start | bytes 442376 | tf_op jit(solution)/shard_map/ppermute | solution.py:308
  143.6 7.6 %collective-permute-start.15 = (bf16[576,256]{1,0:T(8,128)(2,1)S(1)}, bf16[576,256]{1,0:T(8,128)(2,1)S(1)}, u32[]{:S(2)}, u32[]{:S(2)}) collective-permute-start(bf16[576,256]{1,0:T(8,128)(2,1)S(1)} %pad_maximum_fusion.1), channel_id=1, source_target_pairs={{0,4},{1,5},{2,6},{3,7},{4,0},{5,1},{6,2},{7,3},{8,12},{9,13},{10,... | collective-permute-start | bytes 884744 | tf_op jit(solution)/shard_map/ppermute | solution.py:308
  144.0 10.7 %collective-permute-start.16 = (bf16[576,256]{1,0:T(8,128)(2,1)S(1)}, bf16[576,256]{1,0:T(8,128)(2,1)S(1)}, u32[]{:S(2)}, u32[]{:S(2)}) collective-permute-start(bf16[576,256]{1,0:T(8,128)(2,1)S(1)} %pad_maximum_fusion.1), channel_id=1, source_target_pairs={{0,2},{1,3},{2,0},{3,1},{4,6},{5,7},{6,4},{7,5},{8,10},{9,11},{10,... | collective-permute-start | bytes 884744 | tf_op jit(solution)/shard_map/ppermute | solution.py:308
  144.5 10.2 %collective-permute-start.17 = (bf16[576,256]{1,0:T(8,128)(2,1)S(1)}, bf16[576,256]{1,0:T(8,128)(2,1)S(1)}, u32[]{:S(2)}, u32[]{:S(2)}) collective-permute-start(bf16[576,256]{1,0:T(8,128)(2,1)S(1)} %pad_maximum_fusion.1), channel_id=1, source_target_pairs={{0,6},{1,7},{2,4},{3,5},{4,2},{5,3},{6,0},{7,1},{8,14},{9,15},{10,... | collective-permute-start | bytes 884744 | tf_op jit(solution)/shard_map/ppermute | solution.py:308
  154.7 9.0 %copy-start.1 = (bf16[1,12,14,14,256]{4,3,2,1,0:T(8,128)(2,1)S(1)}, bf16[1,12,14,14,256]{4,3,2,1,0:T(8,128)(2,1)}, u32[]{:S(2)}) copy-start(bf16[1,12,14,14,256]{4,3,2,1,0:T(8,128)(2,1)} %param.7) | copy-start | bytes 3612676
  154.8 2.9 %copy-start.4 = (bf16[2304,256]{1,0:T(8,128)(2,1)}, bf16[2304,256]{1,0:T(8,128)(2,1)S(1)}, u32[]{:S(2)}) copy-start(bf16[2304,256]{1,0:T(8,128)(2,1)S(1)} %constant_dynamic-update-slice_fusion.own_ref) | copy-start | bytes 3538948
  154.8 2.9 %collective-permute-start.18 = (bf16[2304,256]{1,0:T(8,128)(2,1)S(1)}, bf16[2304,256]{1,0:T(8,128)(2,1)S(1)}, u32[]{:S(2)}, u32[]{:S(2)}) collective-permute-start(bf16[2304,256]{1,0:T(8,128)(2,1)S(1)} %constant_dynamic-update-slice_fusion.own_ref), channel_id=1, source_target_pairs={{0,1},{1,0},{2,3},{3,2},{4,5},{5,4},{6,7},{7,6},{8,9},{9,8},{10,11... | collective-permute-start | bytes 3538952 | tf_op jit(solution)/shard_map/ppermute | solution.py:308
  157.7 1.0 copy-start.5
  (1 other events, 0.7 us)
